TPU v7x, 32 devices: a whole 2x2x4 slice. The times are simulated.
32 devices in a mesh: groups: 2 (over x), space: 16 (over z, y, core).
Axes of the slice: x: 2, y: 2, z: 4, core: 2. Of those that a mesh axis runs over, the one named last changes fastest.
Arguments:
- eigvecs: bfloat16 [2, 384, 3, 12288], P(None, None, None, ('groups', 'space')), parts along dimension 3, may hold values from -1.5 to 1.5
- momenta: int32 [4, 3], replicated, may hold values from -2 to 2
- peram: bfloat16 [32, 2, 384, 384], P(('groups', 'space')), parts along dimension 0, may hold values from -0.21875 to 0.21875
- graph: int32 [3072, 8], P(('groups', 'space')), parts along dimension 0, may hold values from 0 to 15, all different within a row; in each aligned block of 96 rows (0 to 95, 96 to 191, ...) at most 96 rows name the same one
Outputs:
- contracted: bfloat16 [3072, 8, 768], P(('groups', 'space')), parts along dimension 0
There are 2 independent parts, one for each index of `groups`. A program takes and returns all parts, laid end to end along the dimension named above; an argument that names none is the same for every part. Nothing has to cross between parts.
Inputs may be any that keep to these rules, and one draw needn't show every extreme that they name: `graph`: each row names 8 different owners; among the rows of one device no owner is named more than 96 times, a bound that some block reaches.
All inputs are finite; a program needn't handle non-finite values.
Results may differ from a plain program's by a relative error of at most 0.0064.
Values may be sent and summed in bfloat16 or wider, within the bound.
A program may use at most 64 MiB of HBM per device.

v0:
```python
import functools
import math

import jax
import jax.numpy as jnp
from jax import lax
from jax.experimental import pallas as pl
from jax.experimental.pallas import tpu as pltpu
from jax.sharding import PartitionSpec as P

EXTENT = 128
VMEM_ROOM = 40 << 20
BF16 = jnp.bfloat16
F32 = jnp.float32


def partner(block, axis, bit):
    count = lax.axis_size(axis)
    route = []
    for low in range(count):
        high = low | 1 << bit
        if high != low and high < count:
            route += [(low, high), (high, low)]
    return lax.ppermute(block, axis, route)


def phase_tables(momenta, site_index, extent):
    coord_x = site_index % extent
    coord_y = site_index // extent % extent
    coord_z = site_index // (extent * extent)
    wave_number = (
        momenta[:, 0:1] * coord_x[None, :]
        + momenta[:, 1:2] * coord_y[None, :]
        + momenta[:, 2:3] * coord_z[None, :]
    )
    wave_number = jnp.mod(wave_number, extent)
    phase_angle = wave_number.astype(jnp.float32) * (2.0 * math.pi / extent)
    return (jnp.cos(phase_angle), jnp.sin(phase_angle))


def block_form(peram_pair):
    peram_re = peram_pair[0]
    peram_im = peram_pair[1]
    top_half = jnp.concatenate([peram_re, peram_im], axis=1)
    bottom_half = jnp.concatenate([-peram_im, peram_re], axis=1)
    return jnp.concatenate([top_half, bottom_half], axis=0)


def sink_product(arrived, block):
    return lax.dot_general(
        arrived, block, (((2,), (0,)), ((), ())), preferred_element_type=jnp.float32
    ).astype(jnp.bfloat16)


def adjoint_product(sinks, block):
    return lax.dot_general(
        sinks, block, (((2,), (1,)), ((), ())), preferred_element_type=jnp.float32
    ).astype(jnp.bfloat16)


def on_device(eigvecs, momenta, peram, graph):
    num_vec = eigvecs.shape[1]
    local_sites = eigvecs.shape[3]
    spaces = lax.axis_size("space")
    position = lax.axis_index("space")
    site_index = position * local_sites + jnp.arange(local_sites, dtype=jnp.int32)
    cosine, sine = phase_tables(momenta, site_index, EXTENT)
    total_rows = cosine.shape[0] * num_vec
    rows_here = total_rows // spaces
    right_side = jnp.concatenate(
        [
            jnp.concatenate([eigvecs[0], -eigvecs[1]], axis=1),
            jnp.concatenate([eigvecs[1], eigvecs[0]], axis=1),
        ],
        axis=0,
    ).reshape(2 * num_vec, 6 * local_sites)
    row_index = jnp.arange(rows_here * lax.axis_size("space"), dtype=jnp.int32)
    vector_index = row_index % num_vec
    momentum_index = row_index // num_vec
    vec_re = jnp.take(eigvecs[0], vector_index, axis=0).astype(jnp.float32)
    vec_im = jnp.take(eigvecs[1], vector_index, axis=0).astype(jnp.float32)
    cos_rows = jnp.take(cosine, momentum_index, axis=0)[:, None, :]
    sin_rows = jnp.take(sine, momentum_index, axis=0)[:, None, :]
    left_re = vec_re * cos_rows - vec_im * sin_rows
    left_im = -(vec_re * sin_rows + vec_im * cos_rows)
    left_cat = (
        jnp.concatenate([left_re, left_im], axis=1)
        .astype(jnp.bfloat16)
        .reshape(rows_here * lax.axis_size("space"), 6 * local_sites)
    )
    summed = lax.psum_scatter(
        lax.dot_general(
            left_cat, right_side, (((1,), (1,)), ((), ())), preferred_element_type=jnp.float32
        ),
        "space",
        scatter_dimension=0,
        tiled=True,
    )
    elemental = summed.astype(jnp.bfloat16)
    fanout = graph.shape[1]
    capacity = max(2, 2 * rows_here * fanout // spaces)
    flat_owner = graph.reshape(-1)
    entries = flat_owner.shape[0]
    onehot = (flat_owner[:, None] == jnp.arange(spaces, dtype=jnp.int32)[None, :]).astype(jnp.int32)
    earlier = jnp.cumsum(onehot, axis=0) - onehot
    slot = jnp.sum(earlier * onehot, axis=1)
    source_row = jnp.arange(entries, dtype=jnp.int32) // fanout
    payload = jnp.take(elemental, source_row, axis=0)
    outgoing = (
        jnp.zeros((spaces, capacity, 2 * num_vec), jnp.bfloat16).at[flat_owner, slot].set(payload)
    )
    own_block = block_form(peram[0])
    partner_block = partner(own_block, "space", 0)
    sinks = sink_product(
        lax.all_to_all(outgoing, "space", split_axis=0, concat_axis=0, tiled=True), own_block
    )
    finished = adjoint_product(sinks, partner_block)
    returned = lax.all_to_all(finished, "space", split_axis=0, concat_axis=0, tiled=True)
    collected = returned[flat_owner, slot]
    return collected.reshape(rows_here, fanout, 2 * num_vec)


NT = (((1,), (1,)), ((), ()))
NN = (((1,), (0,)), ((), ()))


def dot(a, b, dims):
    return lax.dot_general(a, b, dims, preferred_element_type=F32)


def fused_kernel(
    lines, wide, vec_ref, cos_ref, sin_ref, peram_ref, owner_ref, out_ref,
    pair, gath, prod, own, core_out, core_in, z_out, z_in, total, y_out, y_in, elem, results, picks,
    pair_sem, core_sem, z_sem, y_sem, gath_send, gath_recv,
):
    colours, num_vec = vec_ref.shape[1:3]
    rows = own.shape[1]
    half = num_vec // 2
    me = lax.axis_index("space")
    core = me % 2
    chip = me // 2
    line = chip // wide
    column = chip % wide
    mate = chip * 2 + 1 - core
    other = 1 - column
    across = (line * wide + other) * 2 + core
    above = me + 2 * wide
    below = me - 2 * wide
    has_above = line < lines - 1
    has_below = line > 0

    def copy(src, dst, send, recv, to):
        return pltpu.make_async_remote_copy(
            src_ref=src, dst_ref=dst, send_sem=send, recv_sem=recv,
            device_id={"space": to}, device_id_type=pl.DeviceIdType.MESH,
        )

    barrier = pltpu.get_barrier_semaphore()

    def greet(to):
        pl.semaphore_signal(barrier, inc=1, device_id={"space": to}, device_id_type=pl.DeviceIdType.MESH)

    greet(mate)
    greet(across)

    @pl.when(has_above)
    def _():
        greet(above)

    @pl.when(has_below)
    def _():
        greet(below)

    def core_copy(unit):
        return copy(core_out.at[unit], core_in.at[unit], core_sem.at[0, unit], core_sem.at[1, unit], mate)

    def unit_product(unit):
        first = unit * (2 * rows)
        momentum = first // num_vec
        start = pl.multiple_of(first % num_vec, 2 * rows)
        cosine = cos_ref[pl.ds(momentum, 1), :]
        sine = sin_ref[pl.ds(momentum, 1), :]
        left = []
        for colour in range(colours):
            v_re = vec_ref[0, colour, pl.ds(start, 2 * rows), :].astype(F32)
            v_im = vec_ref[1, colour, pl.ds(start, 2 * rows), :].astype(F32)
            left_re = (v_re * cosine - v_im * sine).astype(BF16)
            left_im = (-(v_re * sine + v_im * cosine)).astype(BF16)
            left.append(jnp.concatenate([left_re, left_im], axis=0))
        left = jnp.concatenate(left, axis=1)
        by_re = dot(left, jnp.concatenate([vec_ref[0, colour] for colour in range(colours)], axis=1), NT)
        by_im = dot(left, jnp.concatenate([vec_ref[1, colour] for colour in range(colours)], axis=1), NT)
        prod[:, :num_vec] = by_re[: 2 * rows] - by_im[2 * rows :]
        prod[:, num_vec:] = by_im[: 2 * rows] + by_re[2 * rows :]
        own[unit] = prod[pl.ds(pl.multiple_of(core * rows, rows), rows), :]
        core_out[unit] = prod[pl.ds(pl.multiple_of((1 - core) * rows, rows), rows), :].astype(BF16)

    def line_product(to_line):
        @pl.loop(0, wide)
        def _(col):
            unit_product(to_line * wide + col)
            core_copy(to_line * wide + col).start()

    lower = line < lines // 2

    def line_at(step):
        if step == lines - 1:
            return line
        down = lines - 1 - step
        down = jnp.where(down <= line, down - 1, down)
        up = jnp.where(step >= line, step + 1, step)
        return jnp.where(lower, down, up)

    def z_copy(to_line, col, to):
        way = jnp.where(to_line > line, 0, 1)
        return z_arrival(way, to_line, col, to)

    def z_arrival(way, to_line, col, to):
        return copy(
            z_out.at[to_line, col], z_in.at[way, to_line, col],
            z_sem.at[0, to_line, col], z_sem.at[1 + way, to_line, col], to,
        )

    def chip_sum(to_line, col):
        unit = to_line * wide + col
        core_copy(unit).wait_recv()
        return own[unit] + core_in[unit].astype(F32)

    def begin_line(step):
        to_line = line_at(step)
        upward = to_line > line
        first = jnp.where(upward, line == 0, line == lines - 1)

        @pl.when(first)
        def _():
            for col in range(wide):
                z_out[to_line, col] = chip_sum(to_line, col).astype(BF16)
                z_copy(to_line, col, jnp.where(upward, above, below)).start()

    def pass_on(step):
        to_line = line_at(step)
        upward = to_line > line
        way = jnp.where(upward, 0, 1)
        behind = jnp.where(upward, line > 0, line < lines - 1)

        @pl.when(behind)
        def _():
            for col in range(wide):
                z_arrival(way, to_line, col, mate).wait_recv()
                z_out[to_line, col] = (chip_sum(to_line, col) + z_in[way, to_line, col].astype(F32)).astype(BF16)
                z_copy(to_line, col, jnp.where(upward, above, below)).start()

    parts = gath.shape[2]

    def gather_copy(block, which, part, way, to):
        return copy(
            gath.at[block, which, part], gath.at[block, which, part],
            gath_send.at[way, block, part], gath_recv.at[block, which, part], to,
        )

    def gather_arrived(block, which, part):
        gather_copy(block, which, part, 0, mate).wait_recv()

    def forward(distance, part):
        low = line - distance
        high = line + distance

        @pl.when(low >= 0)
        def _():
            block = low * wide + column
            gather_arrived(block, core, part)

            @pl.when(has_above)
            def _():
                gather_copy(block, core, part, 0, above).start()

            gather_copy(block, core, part, 1, across).start()
            gather_copy(block, core, part, 2, mate).start()

        @pl.when(high < lines)
        def _():
            block = high * wide + column
            gather_arrived(block, core, part)

            @pl.when(has_below)
            def _():
                gather_copy(block, core, part, 0, below).start()

            gather_copy(block, core, part, 1, across).start()
            gather_copy(block, core, part, 2, mate).start()

    def relay(at):
        for part in range(parts):
            gather_arrived(at * wide + other, core, part)
            gather_copy(at * wide + other, core, part, 2, mate).start()

    def from_mate(block):
        for part in range(parts):
            gather_arrived(block, 1 - core, part)

    toward = 1 - 2 * (line // (lines // 2))

    def line_on(turn):
        return (line + toward * turn + lines) % lines

    group = results.shape[2]
    fanout = out_ref.shape[1]
    owners = results.shape[1]

    def make_picks():
        spread = lax.broadcasted_iota(jnp.int32, (rows * fanout, fanout), 0) % fanout
        spread = jnp.where(spread == lax.broadcasted_iota(jnp.int32, (rows * fanout, fanout), 1), 1.0, 0.0)
        named = dot(spread.astype(BF16), owner_ref[...].astype(F32).astype(BF16), NN)
        own_row = lax.broadcasted_iota(jnp.int32, named.shape, 0) // fanout
        at_row = own_row == lax.broadcasted_iota(jnp.int32, named.shape, 1)
        named = jnp.sum(jnp.where(at_row, named, 0.0), axis=1, keepdims=True)
        shape = (group * fanout, owners * group)
        of_row = lax.broadcasted_iota(jnp.int32, shape, 0) // fanout
        of_col = lax.broadcasted_iota(jnp.int32, shape, 1)
        same = of_row == of_col % group
        col_owner = (of_col // group).astype(F32)
        for g in range(rows // group):
            chosen = named[g * group * fanout : (g + 1) * group * fanout, :] == col_owner
            picks[g] = jnp.where(same & chosen, 1.0, 0.0).astype(BF16)

    unit_product(line_at(0) * wide)
    peers = 2 + jnp.where(has_above, 1, 0) + jnp.where(has_below, 1, 0)
    pl.semaphore_wait(barrier, peers)

    pair_copy = copy(peram_ref, pair.at[core], pair_sem.at[0], pair_sem.at[1], mate)
    pair_copy.start()
    pair[core] = peram_ref[...]
    core_copy(line_at(0) * wide).start()

    @pl.loop(1, wide)
    def _(col):
        unit_product(line_at(0) * wide + col)
        core_copy(line_at(0) * wide + col).start()

    pair_copy.wait_recv()
    mine_rows = pl.ds(pl.multiple_of(core * half, half), half)
    lefts = jnp.concatenate([pair[0, 0, mine_rows, :], pair[0, 1, mine_rows, :]], axis=0)
    by_re = dot(lefts, pair[1, 0], NT)
    by_im = dot(lefts, pair[1, 1], NT)
    gath[chip, core, 0] = (by_re[:half] + by_im[half:]).astype(BF16)
    gath[chip, core, 1] = (by_re[half:] - by_im[:half]).astype(BF16)
    for part in range(parts):

        @pl.when(has_above)
        def _():
            gather_copy(chip, core, part, 0, above).start()

        @pl.when(has_below)
        def _():
            gather_copy(chip, core, part, 3, below).start()

        gather_copy(chip, core, part, 1, across).start()
        gather_copy(chip, core, part, 2, mate).start()

    for step in range(1, lines):
        if step == lines - 1:
            forward(1, 0)
        line_product(line_at(step))
        begin_line(step - 1)
    for part in range(1, parts):
        forward(1, part)
    relay(line)
    for step in range(1, lines):
        if step < lines - 1:
            for part in range(parts):
                forward(step + 1, part)
            pass_on(step - 1)
    for turn in range(1, lines - 2):
        relay(line_on(turn))
    pass_on(lines - 2)
    for col in range(wide):
        total[col] = chip_sum(line, col)

    @pl.when(has_below)
    def _():
        for col in range(wide):
            z_arrival(0, line, col, mate).wait_recv()
            total[col] += z_in[0, line, col].astype(F32)

    @pl.when(has_above)
    def _():
        for col in range(wide):
            z_arrival(1, line, col, mate).wait_recv()
            total[col] += z_in[1, line, col].astype(F32)

    y_out[...] = total[other].astype(BF16)
    y_copy = copy(y_out, y_in, y_sem.at[0], y_sem.at[1], across)
    y_copy.start()
    make_picks()
    for turn in range(max(1, lines - 2), lines - 1):
        relay(line_on(turn))
    y_copy.wait_recv()
    row = (total[column] + y_in[...].astype(F32)).astype(BF16)
    elem[:rows] = row[:, :num_vec]
    elem[rows:] = row[:, num_vec:]

    def put(owner, re, im):
        sixteen = results.shape[2]
        results[:, owner, :, :num_vec] = re.astype(BF16).reshape(rows // sixteen, sixteen, num_vec)
        results[:, owner, :, num_vec:] = im.astype(BF16).reshape(rows // sixteen, sixteen, num_vec)

    def contract(block):
        m_re = jnp.concatenate([gath[block, 0, 0], gath[block, 1, 0]], axis=0)
        m_im = jnp.concatenate([gath[block, 0, 1], gath[block, 1, 1]], axis=0)
        e = elem[...]
        by_re = dot(e, m_re, NN)
        by_im = dot(e, m_im, NN)
        put(2 * block, by_re[:rows] - by_im[rows:], by_im[:rows] + by_re[rows:])
        by_re = dot(e, m_re, NT)
        by_im = dot(e, m_im, NT)
        put(2 * block + 1, by_re[:rows] + by_im[rows:], by_re[rows:] - by_im[:rows])

    @pl.loop(0, lines)
    def _(turn):
        at = line_on(turn)
        mine = at * wide + column
        theirs = at * wide + other

        @pl.when(turn == 1)
        def _():
            relay(line_on(lines - 1))

        from_mate(mine)
        contract(mine)
        from_mate(theirs)
        contract(theirs)

    for g in range(rows // group):
        rows_out = dot(picks[g], results[g].reshape(owners * group, 2 * num_vec), NN)
        out_ref[g * group : (g + 1) * group] = rows_out.reshape(group, fanout, 2 * num_vec).astype(BF16)

    pair_copy.wait_send()
    y_copy.wait_send()

    @pl.loop(0, lines * wide)
    def _(unit):
        core_copy(unit).wait_send()
        for part in range(parts):
            gather_copy(unit, core, part, 2, mate).wait_send()

    @pl.loop(0, lines)
    def _(at):
        @pl.when(at != line)
        def _():
            for col in range(wide):
                z_copy(at, col, mate).wait_send()

        for part in range(parts):
            gather_copy(at * wide + column, core, part, 1, across).wait_send()

        @pl.when(((at <= line) & has_above) | ((at > line) & has_below))
        def _():
            for part in range(parts):
                gather_copy(at * wide + column, core, part, 0, above).wait_send()

    @pl.when(has_below)
    def _():
        for part in range(parts):
            gather_copy(chip, core, part, 3, below).wait_send()


def fused_on_device(eigvecs, momenta, peram, graph):
    num_vec, colours, local_sites = eigvecs.shape[1:]
    spaces = lax.axis_size("space")
    wide = 2
    lines = spaces // (2 * wide)
    chips = lines * wide
    rows, fanout = graph.shape
    group = 16
    position = lax.axis_index("space")
    site_index = position * local_sites + jnp.arange(local_sites, dtype=jnp.int32)
    cosine, sine = phase_tables(momenta, site_index, EXTENT)
    vectors = jnp.transpose(eigvecs, (0, 2, 1, 3))
    half = num_vec // 2
    dma = pltpu.SemaphoreType.DMA
    return pl.pallas_call(
        functools.partial(fused_kernel, lines, wide),
        out_shape=jax.ShapeDtypeStruct((rows, fanout, 2 * num_vec), BF16),
        in_specs=[pl.BlockSpec(memory_space=pltpu.VMEM)] * 5,
        out_specs=pl.BlockSpec(memory_space=pltpu.VMEM),
        scratch_shapes=[
            pltpu.VMEM((2, 2, num_vec, num_vec), BF16),
            pltpu.VMEM((chips, 2, 2, half, num_vec), BF16),
            pltpu.VMEM((2 * rows, 2 * num_vec), F32),
            pltpu.VMEM((chips, rows, 2 * num_vec), F32),
            pltpu.VMEM((chips, rows, 2 * num_vec), BF16),
            pltpu.VMEM((chips, rows, 2 * num_vec), BF16),
            pltpu.VMEM((lines, wide, rows, 2 * num_vec), BF16),
            pltpu.VMEM((2, lines, wide, rows, 2 * num_vec), BF16),
            pltpu.VMEM((wide, rows, 2 * num_vec), F32),
            pltpu.VMEM((rows, 2 * num_vec), BF16),
            pltpu.VMEM((rows, 2 * num_vec), BF16),
            pltpu.VMEM((2 * rows, num_vec), BF16),
            pltpu.VMEM((rows // group, spaces, group, 2 * num_vec), BF16),
            pltpu.VMEM((rows // group, group * fanout, spaces * group), BF16),
            dma((2,)),
            dma((2, chips)),
            dma((3, lines, wide)),
            dma((2,)),
            dma((4, chips, 2)),
            dma((chips, 2, 2)),
        ],
        compiler_params=pltpu.CompilerParams(
            collective_id=0, has_side_effects=True, vmem_limit_bytes=VMEM_ROOM + (16 << 20)
        ),
    )(vectors, cosine, sine, peram[0], graph.T)


def fits(mesh, eigvecs, momenta, graph):
    num_vec = eigvecs.shape[1]
    spaces = mesh.shape["space"]
    rows = momenta.shape[0] * num_vec // spaces
    return (
        spaces % 8 == 0
        and spaces <= 256
        and rows % 16 == 0
        and num_vec % (2 * rows) == 0
        and num_vec % 128 == 0
        and spaces * 2 * num_vec * num_vec + 14 * spaces * rows * 2 * num_vec <= VMEM_ROOM
    )


def solution(mesh):
    placed = (
        P(None, None, None, ("groups", "space")),
        P(),
        P(("groups", "space"), None, None, None),
        P(("groups", "space"), None),
    )

    def whole(eigvecs, momenta, peram, graph):
        body = fused_on_device if fits(mesh, eigvecs, momenta, graph) else on_device
        return jax.shard_map(
            body,
            mesh=mesh,
            in_specs=placed,
            out_specs=P(("groups", "space"), None, None),
            check_vma=False,
        )(eigvecs, momenta, peram, graph)

    return whole
```

profile of v0, /device:TPU:0, one launch (start us, length us, event | category | flops | bytes accessed | tf_op | source)
XLA Modules:
  0.0 53.1 jit_solution(18272466486416494831)
XLA Ops:
  0.0 1.0 %slice_reduce_fusion.2 = (s32[4]{0:T(128)S(1)}, s32[4]{0:T(128)S(1)}, s32[4]{0:T(128)S(1)}) fusion(s32[4,3]{1,0:T(4,128)} %param.5), kind=kLoop, calls=%fused_computation.24 | loop fusion | bytes 96 | tf_op jit(solution)/shard_map/slice | solution.py:32
  1.1 0.7 %fusion.8 = (f32[4,384]{1,0:T(4,128)}, f32[4,384]{1,0:T(4,128)}) fusion(s32[384]{0:T(512)S(1)} %get-tuple-element.10, s32[4]{0:T(128)S(1)} %get-tuple-element.6, s32[384]{0:T(512)S(1)} %get-tuple-element.11, s32[4]{0:T(128)S(1)} %get-tuple-element.7, s32[384]{0:T(512)S(1)} %add_select_fusion.4, s32[4]{0:T(128)S(1)} %get-tuple-element.5), kind=kLoop, calls=%fused_computation.27 | loop fusion | flops 27648 | bytes 16944 | tf_op jit(solution)/shard_map/sin | solution.py:38
  1.8 48.9 %shard_map.46 = bf16[96,8,768]{2,1,0:T(8,128)(2,1)} custom-call(bf16[2,3,384,384]{3,2,1,0:T(8,128)(2,1)} %bitcast.3, f32[4,384]{1,0:T(4,128)} %get-tuple-element.9.cos_ref, f32[4,384]{1,0:T(4,128)} %get-tuple-element.8.sin_ref, bf16[2,384,384]{2,1,0:T(8,128)(2,1)} %bitcast.4, s32[8,96]{1,0:T(8,128)} %bitcast.5), custom_call_target="tpu_custom_call" | custom-call | tf_op jit(solution)/shard_map/pallas_call | solution.py:481
  50.7 2.4 %copy.6 = bf16[96,8,768]{2,1,0:T(8,128)(2,1)} copy(bf16[96,8,768]{2,1,0:T(8,128)(2,1)} %shard_map.46) | data formatting | bytes 2359296
  (2 shorter events, 0.0 us)
where the time goes:
time: 53.3 us; the launch traced here: 53.1 us
  Pallas kernels  48.9 us (92%)
  local copies, waits for them, and re-layouts  3.37 us (6%)
  other arithmetic  0.78 us (1%)
    pallas_call x1, Pallas kernels, fused_on_device(): pl.pallas_call(functools.partial(fused_kernel, lines, wide), out_shape=ja...  48.9 us
    unnamed x1, local copies, waits for them, and re-layouts  2.36 us

commit v1 on v0

--- a/solution.py
+++ b/solution.py
@@ -128,12 +128,27 @@
     return lax.dot_general(a, b, dims, preferred_element_type=F32)
 
 
+def fill_phases(mom_ref, cos_ref, sin_ref, first_site):
+    count = cos_ref.shape[0]
+    shape = (1, cos_ref.shape[1])
+    bits = EXTENT.bit_length() - 1
+    site = first_site + lax.broadcasted_iota(jnp.int32, shape, 1)
+    coord_x = site & (EXTENT - 1)
+    coord_y = (site >> bits) & (EXTENT - 1)
+    coord_z = site >> (2 * bits)
+    for q in range(count):
+        wave = (mom_ref[q, 0] * coord_x + mom_ref[q, 1] * coord_y + mom_ref[q, 2] * coord_z) & (EXTENT - 1)
+        angle = wave.astype(F32) * (2.0 * math.pi / EXTENT)
+        cos_ref[q : q + 1, :] = jnp.cos(angle)
+        sin_ref[q : q + 1, :] = jnp.sin(angle)
+
+
 def fused_kernel(
-    lines, wide, vec_ref, cos_ref, sin_ref, peram_ref, owner_ref, out_ref,
-    pair, gath, prod, own, core_out, core_in, z_out, z_in, total, y_out, y_in, elem, results, picks,
-    pair_sem, core_sem, z_sem, y_sem, gath_send, gath_recv,
+    lines, wide, mom_ref, vec_hbm, peram_hbm, owner_ref, out_ref,
+    vec_ref, cos_ref, sin_ref, pair, gath, prod, own, core_out, core_in, z_out, z_in, total, y_out, y_in, elem, results, picks,
+    load_sem, pair_sem, core_sem, z_sem, y_sem, gath_send, gath_recv,
 ):
-    colours, num_vec = vec_ref.shape[1:3]
+    colours, num_vec, local_sites = vec_ref.shape[1:]
     rows = own.shape[1]
     half = num_vec // 2
     me = lax.axis_index("space")
@@ -162,6 +177,10 @@
 
     greet(mate)
     greet(across)
+    load_own = pltpu.make_async_copy(peram_hbm, pair.at[core], load_sem.at[0])
+    load_own.start()
+    load_vec = pltpu.make_async_copy(vec_hbm, vec_ref, load_sem.at[1])
+    load_vec.start()
 
     @pl.when(has_above)
     def _():
@@ -323,13 +342,13 @@
             chosen = named[g * group * fanout : (g + 1) * group * fanout, :] == col_owner
             picks[g] = jnp.where(same & chosen, 1.0, 0.0).astype(BF16)
 
-    unit_product(line_at(0) * wide)
+    fill_phases(mom_ref, cos_ref, sin_ref, me * local_sites)
     peers = 2 + jnp.where(has_above, 1, 0) + jnp.where(has_below, 1, 0)
     pl.semaphore_wait(barrier, peers)
-
-    pair_copy = copy(peram_ref, pair.at[core], pair_sem.at[0], pair_sem.at[1], mate)
+    pair_copy = copy(peram_hbm, pair.at[core], pair_sem.at[0], pair_sem.at[1], mate)
     pair_copy.start()
-    pair[core] = peram_ref[...]
+    load_vec.wait()
+    unit_product(line_at(0) * wide)
     core_copy(line_at(0) * wide).start()
 
     @pl.loop(1, wide)
@@ -337,6 +356,7 @@
         unit_product(line_at(0) * wide + col)
         core_copy(line_at(0) * wide + col).start()
 
+    load_own.wait()
     pair_copy.wait_recv()
     mine_rows = pl.ds(pl.multiple_of(core * half, half), half)
     lefts = jnp.concatenate([pair[0, 0, mine_rows, :], pair[0, 1, mine_rows, :]], axis=0)
@@ -472,18 +492,23 @@
     chips = lines * wide
     rows, fanout = graph.shape
     group = 16
-    position = lax.axis_index("space")
-    site_index = position * local_sites + jnp.arange(local_sites, dtype=jnp.int32)
-    cosine, sine = phase_tables(momenta, site_index, EXTENT)
     vectors = jnp.transpose(eigvecs, (0, 2, 1, 3))
     half = num_vec // 2
     dma = pltpu.SemaphoreType.DMA
     return pl.pallas_call(
         functools.partial(fused_kernel, lines, wide),
-        out_shape=jax.ShapeDtypeStruct((rows, fanout, 2 * num_vec), BF16),
-        in_specs=[pl.BlockSpec(memory_space=pltpu.VMEM)] * 5,
+        out_shape=pltpu.VMEM((rows, fanout, 2 * num_vec), BF16),
+        in_specs=[
+            pl.BlockSpec(memory_space=pltpu.SMEM),
+            pl.BlockSpec(memory_space=pltpu.HBM),
+            pl.BlockSpec(memory_space=pltpu.HBM),
+            pl.BlockSpec(memory_space=pltpu.VMEM),
+        ],
         out_specs=pl.BlockSpec(memory_space=pltpu.VMEM),
         scratch_shapes=[
+            pltpu.VMEM((2, colours, num_vec, local_sites), BF16),
+            pltpu.VMEM((momenta.shape[0], local_sites), F32),
+            pltpu.VMEM((momenta.shape[0], local_sites), F32),
             pltpu.VMEM((2, 2, num_vec, num_vec), BF16),
             pltpu.VMEM((chips, 2, 2, half, num_vec), BF16),
             pltpu.VMEM((2 * rows, 2 * num_vec), F32),
@@ -499,6 +524,7 @@
             pltpu.VMEM((rows // group, spaces, group, 2 * num_vec), BF16),
             pltpu.VMEM((rows // group, group * fanout, spaces * group), BF16),
             dma((2,)),
+            dma((2,)),
             dma((2, chips)),
             dma((3, lines, wide)),
             dma((2,)),
@@ -508,7 +534,7 @@
         compiler_params=pltpu.CompilerParams(
             collective_id=0, has_side_effects=True, vmem_limit_bytes=VMEM_ROOM + (16 << 20)
         ),
-    )(vectors, cosine, sine, peram[0], graph.T)
+    )(momenta, vectors, peram[0], graph.T)
 
 
 def fits(mesh, eigvecs, momenta, graph):

time: 53.3 us -> 47.9 us (0.90)
  local copies, waits for them, and re-layouts: 3.37 us -> 1.02 us
  Pallas kernels: 48.9 us -> 46.7 us
  other arithmetic: 0.78 us -> 0 us
    pallas_call x1, Pallas kernels: 48.9 us -> 46.7 us  [fused_on_device(): pl.pallas_call(functools.partial(fused_kernel, lines, wide), out_shape=pl...]
    unnamed x1, local copies, waits for them, and re-layouts: 2.36 us -> 1.02 us
    slice x1 -> x0, local copies, waits for them, and re-layouts: 1.01 us -> none  [phase_tables(): momenta[:, 0:1] * coord_x[None, :] + momenta[:, 1:2] * coord_y[None, :]]
    sin x1 -> x0, other arithmetic: 0.74 us -> none  [phase_tables(): return (jnp.cos(phase_angle), jnp.sin(phase_angle))]
where the time goes in v1:
time: 47.9 us; the launch traced here: 47.7 us
  Pallas kernels  46.7 us (97%)
  local copies, waits for them, and re-layouts  1.02 us (2%)
    pallas_call x1, Pallas kernels, fused_on_device(): pl.pallas_call(functools.partial(fused_kernel, lines, wide), out_shape=pl...  46.7 us
    unnamed x1, local copies, waits for them, and re-layouts  1.02 us

profile of v1, /device:TPU:0, one launch (start us, length us, event | category | flops | bytes accessed | tf_op | source)
XLA Modules:
  0.0 47.7 jit_solution(18297136507778645763)
XLA Ops:
  0.0 46.7 %shard_map.46 = bf16[96,8,768]{2,1,0:T(8,128)(2,1)S(1)} custom-call(s32[4,3]{1,0:T(4,128)} %mom_ref.1, bf16[2,3,384,384]{3,2,1,0:T(8,128)(2,1)} %bitcast.3, bf16[2,384,384]{2,1,0:T(8,128)(2,1)} %bitcast.4, s32[8,96]{1,0:T(8,128)} %bitcast.5), custom_call_target="tpu_custom_call" | custom-call | tf_op jit(solution)/shard_map/pallas_call | solution.py:498
  46.7 1.0 %copy.6 = bf16[96,8,768]{2,1,0:T(8,128)(2,1)} copy(bf16[96,8,768]{2,1,0:T(8,128)(2,1)S(1)} %shard_map.46) | data formatting | bytes 2359296

commit v2 on v1

--- a/solution.py
+++ b/solution.py
@@ -144,9 +144,9 @@
 
 
 def fused_kernel(
-    lines, wide, mom_ref, vec_hbm, peram_hbm, owner_ref, out_ref,
-    vec_ref, cos_ref, sin_ref, pair, gath, prod, own, core_out, core_in, z_out, z_in, total, y_out, y_in, elem, results, picks,
-    load_sem, pair_sem, core_sem, z_sem, y_sem, gath_send, gath_recv,
+    lines, wide, mom_hbm, vec_hbm, peram_hbm, owner_hbm, out_ref,
+    mom_ref, vec_ref, owner_ref, cos_ref, sin_ref, pair, gath, prod, own, core_out, core_in, z_out, z_in, total, y_out, y_in,
+    lhs, results, picks, load_sem, send_sem, pair_recv, core_recv, z_recv, y_recv, gath_recv, mate_recv,
 ):
     colours, num_vec, local_sites = vec_ref.shape[1:]
     rows = own.shape[1]
@@ -177,10 +177,6 @@
 
     greet(mate)
     greet(across)
-    load_own = pltpu.make_async_copy(peram_hbm, pair.at[core], load_sem.at[0])
-    load_own.start()
-    load_vec = pltpu.make_async_copy(vec_hbm, vec_ref, load_sem.at[1])
-    load_vec.start()
 
     @pl.when(has_above)
     def _():
@@ -190,8 +186,19 @@
     def _():
         greet(below)
 
+    loads = [
+        pltpu.make_async_copy(src, dst, load_sem.at[place])
+        for place, (src, dst) in enumerate(
+            [(mom_hbm, mom_ref), (peram_hbm, pair.at[core]), (vec_hbm, vec_ref), (owner_hbm, owner_ref)]
+        )
+    ]
+    for load in loads:
+        load.start()
+    load_mom, load_own, load_vec, load_owner = loads
+    UP, ACROSS, MATE, DOWN, CORES, LINES, TOTALS, PAIR = range(8)
+
     def core_copy(unit):
-        return copy(core_out.at[unit], core_in.at[unit], core_sem.at[0, unit], core_sem.at[1, unit], mate)
+        return copy(core_out.at[unit], core_in.at[unit], send_sem.at[CORES], core_recv.at[unit], mate)
 
     def unit_product(unit):
         first = unit * (2 * rows)
@@ -214,13 +221,11 @@
         own[unit] = prod[pl.ds(pl.multiple_of(core * rows, rows), rows), :]
         core_out[unit] = prod[pl.ds(pl.multiple_of((1 - core) * rows, rows), rows), :].astype(BF16)
 
-    def line_product(to_line):
-        @pl.loop(0, wide)
-        def _(col):
-            unit_product(to_line * wide + col)
-            core_copy(to_line * wide + col).start()
-
     lower = line < lines // 2
+    below_count = line
+    above_count = lines - 1 - line
+    at_end = (line == 0) | (line == lines - 1)
+    toward = jnp.where(lower, 1, -1)
 
     def line_at(step):
         if step == lines - 1:
@@ -230,97 +235,169 @@
         up = jnp.where(step >= line, step + 1, step)
         return jnp.where(lower, down, up)
 
-    def z_copy(to_line, col, to):
-        way = jnp.where(to_line > line, 0, 1)
-        return z_arrival(way, to_line, col, to)
-
-    def z_arrival(way, to_line, col, to):
+    def column_at(piece):
+        return jnp.where(piece == 0, other, column)
+
+    def product_at(step, piece):
+        unit = line_at(step) * wide + column_at(piece)
+        unit_product(unit)
+        core_copy(unit).start()
+
+    share = rows // 2
+
+    def z_copy(way, to_line, col, piece, to):
+        span = pl.ds(piece * share, share)
         return copy(
-            z_out.at[to_line, col], z_in.at[way, to_line, col],
-            z_sem.at[0, to_line, col], z_sem.at[1 + way, to_line, col], to,
+            z_out.at[to_line, col, span], z_in.at[way, to_line, col, span],
+            send_sem.at[LINES], z_recv.at[z_place(way, to_line, line + (1 - 2 * way)), col, piece], to,
         )
 
-    def chip_sum(to_line, col):
+    def z_place(way, to_line, at):
+        return jnp.where(to_line == at, lines, to_line) if way else to_line
+
+    def z_arrived(way, to_line, col, piece):
+        span = pl.ds(piece * share, share)
+        copy(
+            z_out.at[to_line, col, span], z_in.at[way, to_line, col, span],
+            send_sem.at[LINES], z_recv.at[z_place(way, to_line, line), col, piece], mate,
+        ).wait_recv()
+
+    def chip_sum(to_line, col, span):
         unit = to_line * wide + col
-        core_copy(unit).wait_recv()
-        return own[unit] + core_in[unit].astype(F32)
-
-    def begin_line(step):
+        return own[unit, span] + core_in[unit, span].astype(F32)
+
+    def mate_sent(to_line, col):
+        core_copy(to_line * wide + col).wait_recv()
+
+    def spans():
+        return [(piece, pl.ds(piece * share, share)) for piece in range(2)]
+
+    def begin(step, piece):
         to_line = line_at(step)
-        upward = to_line > line
-        first = jnp.where(upward, line == 0, line == lines - 1)
-
-        @pl.when(first)
-        def _():
-            for col in range(wide):
-                z_out[to_line, col] = chip_sum(to_line, col).astype(BF16)
-                z_copy(to_line, col, jnp.where(upward, above, below)).start()
-
-    def pass_on(step):
-        to_line = line_at(step)
-        upward = to_line > line
-        way = jnp.where(upward, 0, 1)
-        behind = jnp.where(upward, line > 0, line < lines - 1)
-
-        @pl.when(behind)
-        def _():
-            for col in range(wide):
-                z_arrival(way, to_line, col, mate).wait_recv()
-                z_out[to_line, col] = (chip_sum(to_line, col) + z_in[way, to_line, col].astype(F32)).astype(BF16)
-                z_copy(to_line, col, jnp.where(upward, above, below)).start()
+        col = column_at(piece)
+
+        def send(way, to):
+            mate_sent(to_line, col)
+            for part, span in spans():
+                z_out[to_line, col, span] = chip_sum(to_line, col, span).astype(BF16)
+                z_copy(way, to_line, col, part, to).start()
+
+        @pl.when(line == 0)
+        def _():
+            send(0, above)
+
+        @pl.when(line == lines - 1)
+        def _():
+            send(1, below)
+
+    def pass_on(way, to_line, piece, to):
+        col = column_at(piece)
+        mate_sent(to_line, col)
+        for part, span in spans():
+            z_arrived(way, to_line, col, part)
+            before = z_in[way, to_line, col, span].astype(F32)
+            z_out[to_line, col, span] = (chip_sum(to_line, col, span) + before).astype(BF16)
+            z_copy(way, to_line, col, part, to).start()
 
     parts = gath.shape[2]
 
-    def gather_copy(block, which, part, way, to):
-        return copy(
-            gath.at[block, which, part], gath.at[block, which, part],
-            gath_send.at[way, block, part], gath_recv.at[block, which, part], to,
-        )
-
-    def gather_arrived(block, which, part):
-        gather_copy(block, which, part, 0, mate).wait_recv()
-
-    def forward(distance, part):
-        low = line - distance
-        high = line + distance
-
-        @pl.when(low >= 0)
-        def _():
-            block = low * wide + column
-            gather_arrived(block, core, part)
+    def gather_copy(block, part, way, to):
+        there = gath.at[block, core, part]
+        recv = mate_recv.at[block] if way == MATE else gath_recv.at[block, part]
+        return copy(there, there, send_sem.at[way], recv, to)
+
+    def gather_arrived(block, part):
+        gather_copy(block, part, ACROSS, across).wait_recv()
+
+    def from_mate(block):
+        there = gath.at[block, 1 - core]
+        copy(there, there, send_sem.at[MATE], mate_recv.at[block], mate).wait_recv()
+
+    def spread(at, part, onward, way, to, hold):
+        block = at * wide + column
+        gather_arrived(block, part)
+
+        @pl.when(onward)
+        def _():
+            gather_copy(block, part, way, to).start()
+
+        @pl.when(jnp.logical_not(hold))
+        def _():
+            gather_copy(block, part, ACROSS, across).start()
+
+        gather_copy(block, part, MATE, mate).start()
+
+    def nth_line(turn):
+        inner = jnp.where(turn == 2, -1, jnp.where(turn == 3, 2, turn))
+        return line + toward * jnp.where(at_end, turn, inner)
+
+    def relay(nth):
+        ends = toward * (nth // 2)
+        inner = [0, 0, -1, 1, toward, 2 * toward, -toward, 2 * toward][nth]
+        part = jnp.where(at_end, nth % 2, [0, 1, 0, 0, 1, 0, 1, 1][nth])
+        block = (line + jnp.where(at_end, ends, inner)) * wide + other
+        gather_arrived(block, part)
+        gather_copy(block, part, MATE, mate).start()
+
+    def arrivals(turn, count):
+        tail = 2 * count - 1
+        first = (turn == tail + 1) | (turn == tail + 2)
+        is_block = (count > 0) & ((turn <= tail) | (turn == tail + 3))
+        back = jnp.where(turn < tail, (turn + 1) // 2, count)
+        ahead = jnp.where(first, lines - 1 - count, lines - (turn + 1) // 2)
+        part = jnp.where(turn <= tail, (turn - 1) % 2, jnp.where(first, turn - tail - 1, jnp.where(turn == tail + 3, 1, (turn - 1) % 2)))
+        is_sum = (count > 0) & jnp.logical_not(is_block) & (ahead > 0)
+        return is_block, is_sum, back, ahead, part
+
+    def held(at, part):
+        return (at == line + toward * jnp.where(at_end, lines - 1, 2)) & (part == jnp.where(at_end, 0, 1))
+
+    def slot(turn):
+        is_block, is_sum, back, ahead, part = arrivals(turn, below_count)
+
+        @pl.when(is_block)
+        def _():
+            spread(line - back, part, has_above, UP, above, held(line - back, part))
+
+        @pl.when(is_sum)
+        def _():
+            pass_on(0, line + ahead, part, above)
+
+        is_block_, is_sum_, back_, ahead_, part_ = arrivals(turn, above_count)
+
+        @pl.when(is_block_)
+        def _():
+            spread(line + back_, part_, has_below, DOWN, below, held(line + back_, part_))
+
+        @pl.when(is_sum_)
+        def _():
+            pass_on(1, line - ahead_, part_, below)
+
+    def line_total(piece, after=None):
+        col = column_at(piece)
+        mate_sent(line, col)
+        for part, span in spans():
+            total[col, span] = chip_sum(line, col, span)
+
+            @pl.when(has_below)
+            def _():
+                z_arrived(0, line, col, part)
+                total[col, span] += z_in[0, line, col, span].astype(F32)
 
             @pl.when(has_above)
             def _():
-                gather_copy(block, core, part, 0, above).start()
-
-            gather_copy(block, core, part, 1, across).start()
-            gather_copy(block, core, part, 2, mate).start()
-
-        @pl.when(high < lines)
-        def _():
-            block = high * wide + column
-            gather_arrived(block, core, part)
-
-            @pl.when(has_below)
-            def _():
-                gather_copy(block, core, part, 0, below).start()
-
-            gather_copy(block, core, part, 1, across).start()
-            gather_copy(block, core, part, 2, mate).start()
-
-    def relay(at):
-        for part in range(parts):
-            gather_arrived(at * wide + other, core, part)
-            gather_copy(at * wide + other, core, part, 2, mate).start()
-
-    def from_mate(block):
-        for part in range(parts):
-            gather_arrived(block, 1 - core, part)
-
-    toward = 1 - 2 * (line // (lines // 2))
-
-    def line_on(turn):
-        return (line + toward * turn + lines) % lines
+                z_arrived(1, line, col, part)
+                total[col, span] += z_in[1, line, col, span].astype(F32)
+
+            if after is not None:
+                after(part, span)
+
+    def y_copy(part, span):
+        return copy(y_out.at[span], y_in.at[span], send_sem.at[TOTALS], y_recv.at[part], across)
+
+    def send_across(part, span):
+        y_out[span] = total[other, span].astype(BF16)
+        y_copy(part, span).start()
 
     group = results.shape[2]
     fanout = out_ref.shape[1]
@@ -342,82 +419,117 @@
             chosen = named[g * group * fanout : (g + 1) * group * fanout, :] == col_owner
             picks[g] = jnp.where(same & chosen, 1.0, 0.0).astype(BF16)
 
+    peers = 2 + jnp.where(has_above, 1, 0) + jnp.where(has_below, 1, 0)
+    with jax.named_scope("greet"):
+        pl.semaphore_wait(barrier, peers)
+    pair_copy = copy(peram_hbm, pair.at[core], send_sem.at[PAIR], pair_recv.at[0], mate)
+    pair_copy.start()
+    load_mom.wait()
     fill_phases(mom_ref, cos_ref, sin_ref, me * local_sites)
-    peers = 2 + jnp.where(has_above, 1, 0) + jnp.where(has_below, 1, 0)
-    pl.semaphore_wait(barrier, peers)
-    pair_copy = copy(peram_hbm, pair.at[core], pair_sem.at[0], pair_sem.at[1], mate)
-    pair_copy.start()
-    load_vec.wait()
-    unit_product(line_at(0) * wide)
-    core_copy(line_at(0) * wide).start()
-
-    @pl.loop(1, wide)
-    def _(col):
-        unit_product(line_at(0) * wide + col)
-        core_copy(line_at(0) * wide + col).start()
-
     load_own.wait()
-    pair_copy.wait_recv()
+    with jax.named_scope("pair"):
+        pair_copy.wait_recv()
     mine_rows = pl.ds(pl.multiple_of(core * half, half), half)
-    lefts = jnp.concatenate([pair[0, 0, mine_rows, :], pair[0, 1, mine_rows, :]], axis=0)
-    by_re = dot(lefts, pair[1, 0], NT)
-    by_im = dot(lefts, pair[1, 1], NT)
-    gath[chip, core, 0] = (by_re[:half] + by_im[half:]).astype(BF16)
-    gath[chip, core, 1] = (by_re[half:] - by_im[:half]).astype(BF16)
+    with jax.named_scope("block"):
+        lefts = jnp.concatenate([pair[0, 0, mine_rows, :], pair[0, 1, mine_rows, :]], axis=0)
+        by_re = dot(lefts, pair[1, 0], NT)
+        by_im = dot(lefts, pair[1, 1], NT)
+        gath[chip, core, 0] = (by_re[:half] + by_im[half:]).astype(BF16)
+        gath[chip, core, 1] = (by_re[half:] - by_im[:half]).astype(BF16)
+    def send_own(part):
+        @pl.when(has_above)
+        def _():
+            gather_copy(chip, part, UP, above).start()
+
+        @pl.when(has_below)
+        def _():
+            gather_copy(chip, part, DOWN, below).start()
+
     for part in range(parts):
-
-        @pl.when(has_above)
-        def _():
-            gather_copy(chip, core, part, 0, above).start()
-
-        @pl.when(has_below)
-        def _():
-            gather_copy(chip, core, part, 3, below).start()
-
-        gather_copy(chip, core, part, 1, across).start()
-        gather_copy(chip, core, part, 2, mate).start()
-
-    for step in range(1, lines):
-        if step == lines - 1:
-            forward(1, 0)
-        line_product(line_at(step))
-        begin_line(step - 1)
-    for part in range(1, parts):
-        forward(1, part)
-    relay(line)
-    for step in range(1, lines):
-        if step < lines - 1:
-            for part in range(parts):
-                forward(step + 1, part)
-            pass_on(step - 1)
-    for turn in range(1, lines - 2):
-        relay(line_on(turn))
-    pass_on(lines - 2)
-    for col in range(wide):
-        total[col] = chip_sum(line, col)
-
-    @pl.when(has_below)
+        gather_copy(chip, part, ACROSS, across).start()
+    send_own(0)
+
+    @pl.when(jnp.logical_not(at_end))
     def _():
-        for col in range(wide):
-            z_arrival(0, line, col, mate).wait_recv()
-            total[col] += z_in[0, line, col].astype(F32)
-
-    @pl.when(has_above)
+        send_own(1)
+
+    for part in range(parts):
+        gather_copy(chip, part, MATE, mate).start()
+
+    def named_product(step, piece):
+        with jax.named_scope(f"unit{step}{piece}"):
+            product_at(step, piece)
+
+    def named_slot(turn):
+        with jax.named_scope(f"slot{turn}"):
+            slot(turn)
+            relay(turn - 1)
+
+    with jax.named_scope("load"):
+        load_vec.wait()
+    named_product(0, 0)
+    named_product(0, 1)
+    begin(0, 0)
+    named_product(1, 0)
+    begin(0, 1)
+
+    @pl.when(at_end)
     def _():
-        for col in range(wide):
-            z_arrival(1, line, col, mate).wait_recv()
-            total[col] += z_in[1, line, col].astype(F32)
-
-    y_out[...] = total[other].astype(BF16)
-    y_copy = copy(y_out, y_in, y_sem.at[0], y_sem.at[1], across)
-    y_copy.start()
-    make_picks()
-    for turn in range(max(1, lines - 2), lines - 1):
-        relay(line_on(turn))
-    y_copy.wait_recv()
+        send_own(1)
+
+    named_slot(1)
+    named_product(1, 1)
+    named_product(2, 0)
+    begin(1, 0)
+    begin(1, 1)
+    named_slot(2)
+    named_product(2, 1)
+    named_product(3, 0)
+    begin(2, 0)
+    begin(2, 1)
+    named_slot(3)
+    named_product(3, 1)
+    load_owner.wait()
+    with jax.named_scope("picks"):
+        make_picks()
+    named_slot(4)
+    named_slot(5)
+    named_slot(6)
+    farthest = nth_line(lines - 1) * wide + column
+
+    @pl.when(at_end)
+    def _():
+        with jax.named_scope("total0"):
+            line_total(0, send_across)
+
+    with jax.named_scope("slot7"):
+        slot(7)
+
+    @pl.when(at_end)
+    def _():
+        with jax.named_scope("total1"):
+            line_total(1)
+        gather_copy(farthest, 0, ACROSS, across).start()
+
+    @pl.when(jnp.logical_not(at_end))
+    def _():
+        with jax.named_scope("total0"):
+            relay(6)
+            line_total(0, send_across)
+        with jax.named_scope("total1"):
+            line_total(1)
+        gather_copy(farthest, 1, ACROSS, across).start()
+
+    with jax.named_scope("across"):
+        for part, span in spans():
+            y_copy(part, span).wait_recv()
     row = (total[column] + y_in[...].astype(F32)).astype(BF16)
-    elem[:rows] = row[:, :num_vec]
-    elem[rows:] = row[:, num_vec:]
+    row_re = row[:, :num_vec]
+    row_im = row[:, num_vec:]
+    lhs[0, :rows] = jnp.concatenate([row_re, -row_im], axis=1)
+    lhs[0, rows:] = jnp.concatenate([row_im, row_re], axis=1)
+    lhs[1, :rows] = row
+    lhs[1, rows:] = jnp.concatenate([row_im, -row_re], axis=1)
 
     def put(owner, re, im):
         sixteen = results.shape[2]
@@ -425,63 +537,57 @@
         results[:, owner, :, num_vec:] = im.astype(BF16).reshape(rows // sixteen, sixteen, num_vec)
 
     def contract(block):
-        m_re = jnp.concatenate([gath[block, 0, 0], gath[block, 1, 0]], axis=0)
-        m_im = jnp.concatenate([gath[block, 0, 1], gath[block, 1, 1]], axis=0)
-        e = elem[...]
-        by_re = dot(e, m_re, NN)
-        by_im = dot(e, m_im, NN)
-        put(2 * block, by_re[:rows] - by_im[rows:], by_im[:rows] + by_re[rows:])
-        by_re = dot(e, m_re, NT)
-        by_im = dot(e, m_im, NT)
-        put(2 * block + 1, by_re[:rows] + by_im[rows:], by_re[rows:] - by_im[:rows])
-
-    @pl.loop(0, lines)
+        high = jnp.concatenate([gath[block, 0, 0], gath[block, 1, 0], gath[block, 0, 1], gath[block, 1, 1]], axis=0)
+        by = dot(lhs[0], high, NN)
+        put(2 * block, by[:rows], by[rows:])
+        broad = [jnp.concatenate([gath[block, which, 0], gath[block, which, 1]], axis=1) for which in range(2)]
+        by = dot(lhs[1], jnp.concatenate(broad, axis=0), NT)
+        put(2 * block + 1, by[:rows], by[rows:])
+
+    @pl.loop(0, 2 * lines)
     def _(turn):
-        at = line_on(turn)
-        mine = at * wide + column
-        theirs = at * wide + other
-
-        @pl.when(turn == 1)
-        def _():
-            relay(line_on(lines - 1))
-
-        from_mate(mine)
-        contract(mine)
-        from_mate(theirs)
-        contract(theirs)
+        @pl.when(at_end & (turn == 2 * lines - 3))
+        def _():
+            with jax.named_scope("slot8"):
+                slot(2 * lines)
+                relay(2 * lines - 2)
+
+        @pl.when(turn == jnp.where(at_end, 2 * lines - 1, 2 * lines - 2))
+        def _():
+            with jax.named_scope("last"):
+                relay(2 * lines - 1)
+
+        late = turn >= 2 * lines - 2
+        near = jnp.where(late, turn % 2 == 0, turn < lines - 1)
+        nth = jnp.where(late, lines - 1, turn % (lines - 1))
+        block = nth_line(nth) * wide + jnp.where(near, column, other)
+        with jax.named_scope("mate"):
+            from_mate(block)
+        with jax.named_scope("contract"):
+            contract(block)
 
     for g in range(rows // group):
         rows_out = dot(picks[g], results[g].reshape(owners * group, 2 * num_vec), NN)
         out_ref[g * group : (g + 1) * group] = rows_out.reshape(group, fanout, 2 * num_vec).astype(BF16)
 
+    def all_sent(what, way):
+        copy(what, what, send_sem.at[way], core_recv.at[0], mate).wait_send()
+
     pair_copy.wait_send()
-    y_copy.wait_send()
-
-    @pl.loop(0, lines * wide)
-    def _(unit):
-        core_copy(unit).wait_send()
-        for part in range(parts):
-            gather_copy(unit, core, part, 2, mate).wait_send()
-
-    @pl.loop(0, lines)
-    def _(at):
-        @pl.when(at != line)
-        def _():
-            for col in range(wide):
-                z_copy(at, col, mate).wait_send()
-
-        for part in range(parts):
-            gather_copy(at * wide + column, core, part, 1, across).wait_send()
-
-        @pl.when(((at <= line) & has_above) | ((at > line) & has_below))
-        def _():
-            for part in range(parts):
-                gather_copy(at * wide + column, core, part, 0, above).wait_send()
-
-    @pl.when(has_below)
-    def _():
-        for part in range(parts):
-            gather_copy(chip, core, part, 3, below).wait_send()
+    all_sent(core_out, CORES)
+    all_sent(z_out.at[pl.ds(0, lines - 1)], LINES)
+    all_sent(y_out, TOTALS)
+    all_sent(gath.at[pl.ds(0, lines), core], ACROSS)
+    all_sent(gath.at[:, core], MATE)
+    for count in range(1, lines):
+
+        @pl.when(line == count - 1)
+        def _():
+            all_sent(gath.at[pl.ds(0, count), core], UP)
+
+        @pl.when(line == lines - count)
+        def _():
+            all_sent(gath.at[pl.ds(0, count), core], DOWN)
 
 
 def fused_on_device(eigvecs, momenta, peram, graph):
@@ -498,15 +604,12 @@
     return pl.pallas_call(
         functools.partial(fused_kernel, lines, wide),
         out_shape=pltpu.VMEM((rows, fanout, 2 * num_vec), BF16),
-        in_specs=[
-            pl.BlockSpec(memory_space=pltpu.SMEM),
-            pl.BlockSpec(memory_space=pltpu.HBM),
-            pl.BlockSpec(memory_space=pltpu.HBM),
-            pl.BlockSpec(memory_space=pltpu.VMEM),
-        ],
+        in_specs=[pl.BlockSpec(memory_space=pltpu.HBM)] * 4,
         out_specs=pl.BlockSpec(memory_space=pltpu.VMEM),
         scratch_shapes=[
+            pltpu.SMEM(momenta.shape, jnp.int32),
             pltpu.VMEM((2, colours, num_vec, local_sites), BF16),
+            pltpu.VMEM((fanout, rows), jnp.int32),
             pltpu.VMEM((momenta.shape[0], local_sites), F32),
             pltpu.VMEM((momenta.shape[0], local_sites), F32),
             pltpu.VMEM((2, 2, num_vec, num_vec), BF16),
@@ -520,16 +623,17 @@
             pltpu.VMEM((wide, rows, 2 * num_vec), F32),
             pltpu.VMEM((rows, 2 * num_vec), BF16),
             pltpu.VMEM((rows, 2 * num_vec), BF16),
-            pltpu.VMEM((2 * rows, num_vec), BF16),
+            pltpu.VMEM((2, 2 * rows, 2 * num_vec), BF16),
             pltpu.VMEM((rows // group, spaces, group, 2 * num_vec), BF16),
             pltpu.VMEM((rows // group, group * fanout, spaces * group), BF16),
+            dma((4,)),
+            dma((8,)),
+            dma((1,)),
+            dma((chips,)),
+            dma((lines + 1, wide, 2)),
             dma((2,)),
-            dma((2,)),
-            dma((2, chips)),
-            dma((3, lines, wide)),
-            dma((2,)),
-            dma((4, chips, 2)),
-            dma((chips, 2, 2)),
+            dma((chips, 2)),
+            dma((chips,)),
         ],
         compiler_params=pltpu.CompilerParams(
             collective_id=0, has_side_effects=True, vmem_limit_bytes=VMEM_ROOM + (16 << 20)
@@ -542,8 +646,7 @@
     spaces = mesh.shape["space"]
     rows = momenta.shape[0] * num_vec // spaces
     return (
-        spaces % 8 == 0
-        and spaces <= 256
+        spaces == 16
         and rows % 16 == 0
         and num_vec % (2 * rows) == 0
         and num_vec % 128 == 0

time: 47.9 us -> 43.4 us (0.906)
  the two profiles are of different devices: /device:TPU:0 before, /device:TPU:1 now
where the time goes in v2:
time: 43.4 us; the launch traced here: 43.2 us
  Pallas kernels  42.2 us (97%)
  local copies, waits for them, and re-layouts  1.02 us (2%)
    pallas_call x1, Pallas kernels, fused_on_device(): pl.pallas_call(functools.partial(fused_kernel, lines, wide), out_shape=pl...  42.2 us
    unnamed x1, local copies, waits for them, and re-layouts  1.02 us

profile of v2, /device:TPU:1, one launch (start us, length us, event | category | flops | bytes accessed | tf_op | source)
XLA Modules:
  0.0 43.2 jit_solution(7473229037478451259)
XLA Ops:
  0.0 42.2 %shard_map.46 = bf16[96,8,768]{2,1,0:T(8,128)(2,1)S(1)} custom-call(s32[4,3]{1,0:T(4,128)} %mom_hbm.1, bf16[2,3,384,384]{3,2,1,0:T(8,128)(2,1)} %bitcast.3, bf16[2,384,384]{2,1,0:T(8,128)(2,1)} %bitcast.4, s32[8,96]{1,0:T(8,128)} %bitcast.5), custom_call_target="tpu_custom_call" | custom-call | tf_op jit(solution)/shard_map/pallas_call | solution.py:604
  42.2 1.0 %copy.6 = bf16[96,8,768]{2,1,0:T(8,128)(2,1)} copy(bf16[96,8,768]{2,1,0:T(8,128)(2,1)S(1)} %shard_map.46) | data formatting | bytes 2359296

commit v3 on v2

--- a/solution.py
+++ b/solution.py
@@ -290,59 +290,64 @@
         def _():
             send(1, below)
 
-    def pass_on(way, to_line, piece, to):
+    def pass_on(way, to_line, piece, part, to, wait):
         col = column_at(piece)
-        mate_sent(to_line, col)
-        for part, span in spans():
-            z_arrived(way, to_line, col, part)
-            before = z_in[way, to_line, col, span].astype(F32)
-            z_out[to_line, col, span] = (chip_sum(to_line, col, span) + before).astype(BF16)
+        if part == 0:
+            mate_sent(to_line, col)
+        span = pl.ds(part * share, share)
+        z_arrived(way, to_line, col, part)
+        before = z_in[way, to_line, col, span].astype(F32)
+        z_out[to_line, col, span] = (chip_sum(to_line, col, span) + before).astype(BF16)
+
+        @pl.when(jnp.logical_not(wait))
+        def _():
             z_copy(way, to_line, col, part, to).start()
 
     parts = gath.shape[2]
 
-    def gather_copy(block, part, way, to):
-        there = gath.at[block, core, part]
-        recv = mate_recv.at[block] if way == MATE else gath_recv.at[block, part]
+    def gather_copy(block, part, piece, way, to):
+        there = gath.at[block, core, part, pl.ds(piece * (half // 2), half // 2)]
+        recv = mate_recv.at[block] if way == MATE else gath_recv.at[block, part, piece]
         return copy(there, there, send_sem.at[way], recv, to)
 
-    def gather_arrived(block, part):
-        gather_copy(block, part, ACROSS, across).wait_recv()
+    def gather_arrived(block, part, piece):
+        gather_copy(block, part, piece, ACROSS, across).wait_recv()
 
     def from_mate(block):
         there = gath.at[block, 1 - core]
         copy(there, there, send_sem.at[MATE], mate_recv.at[block], mate).wait_recv()
 
-    def spread(at, part, onward, way, to, hold):
+    def spread(at, part, piece, onward, way, to):
         block = at * wide + column
-        gather_arrived(block, part)
+        gather_arrived(block, part, piece)
 
         @pl.when(onward)
         def _():
-            gather_copy(block, part, way, to).start()
-
-        @pl.when(jnp.logical_not(hold))
-        def _():
-            gather_copy(block, part, ACROSS, across).start()
-
-        gather_copy(block, part, MATE, mate).start()
+            gather_copy(block, part, piece, way, to).start()
+
+        @pl.when(jnp.logical_not(held(at, part)))
+        def _():
+            gather_copy(block, part, piece, ACROSS, across).start()
+
+        gather_copy(block, part, piece, MATE, mate).start()
 
     def nth_line(turn):
         inner = jnp.where(turn == 2, -1, jnp.where(turn == 3, 2, turn))
         return line + toward * jnp.where(at_end, turn, inner)
 
-    def relay(nth):
+    def relay(nth, piece):
         ends = toward * (nth // 2)
         inner = [0, 0, -1, 1, toward, 2 * toward, -toward, 2 * toward][nth]
         part = jnp.where(at_end, nth % 2, [0, 1, 0, 0, 1, 0, 1, 1][nth])
         block = (line + jnp.where(at_end, ends, inner)) * wide + other
-        gather_arrived(block, part)
-        gather_copy(block, part, MATE, mate).start()
+        gather_arrived(block, part, piece)
+        gather_copy(block, part, piece, MATE, mate).start()
 
     def arrivals(turn, count):
         tail = 2 * count - 1
         first = (turn == tail + 1) | (turn == tail + 2)
-        is_block = (count > 0) & ((turn <= tail) | (turn == tail + 3))
+        last_piece = jnp.where(count == lines - 1, 2, 3)
+        is_block = (count > 0) & ((turn <= tail) | (turn == tail + last_piece))
         back = jnp.where(turn < tail, (turn + 1) // 2, count)
         ahead = jnp.where(first, lines - 1 - count, lines - (turn + 1) // 2)
         part = jnp.where(turn <= tail, (turn - 1) % 2, jnp.where(first, turn - tail - 1, jnp.where(turn == tail + 3, 1, (turn - 1) % 2)))
@@ -350,28 +355,41 @@
         return is_block, is_sum, back, ahead, part
 
     def held(at, part):
-        return (at == line + toward * jnp.where(at_end, lines - 1, 2)) & (part == jnp.where(at_end, 0, 1))
-
-    def slot(turn):
+        return jnp.logical_not(at_end) & (at == line + 2 * toward) & (part == 1)
+
+    def late_sum(turn, count):
+        return (count == lines - 2) & (turn == 2 * lines - 3)
+
+    def send_late(way, count, to_line, to):
+        @pl.when(count == lines - 2)
+        def _():
+            for part in range(2):
+                z_copy(way, to_line, column, part, to).start()
+
+    def slot(turn, piece):
         is_block, is_sum, back, ahead, part = arrivals(turn, below_count)
 
         @pl.when(is_block)
         def _():
-            spread(line - back, part, has_above, UP, above, held(line - back, part))
+            spread(line - back, part, piece, has_above, UP, above)
 
         @pl.when(is_sum)
         def _():
-            pass_on(0, line + ahead, part, above)
+            pass_on(0, line + ahead, part, piece, above, late_sum(turn, below_count))
 
         is_block_, is_sum_, back_, ahead_, part_ = arrivals(turn, above_count)
 
         @pl.when(is_block_)
         def _():
-            spread(line + back_, part_, has_below, DOWN, below, held(line + back_, part_))
+            spread(line + back_, part_, piece, has_below, DOWN, below)
 
         @pl.when(is_sum_)
         def _():
-            pass_on(1, line - ahead_, part_, below)
+            pass_on(1, line - ahead_, part_, piece, below, late_sum(turn, above_count))
+
+        if turn == 2 * lines - 2 and piece == 1:
+            send_late(0, below_count, lines - 1, above)
+            send_late(1, above_count, 0, below)
 
     def line_total(piece, after=None):
         col = column_at(piece)
@@ -422,48 +440,90 @@
     peers = 2 + jnp.where(has_above, 1, 0) + jnp.where(has_below, 1, 0)
     with jax.named_scope("greet"):
         pl.semaphore_wait(barrier, peers)
-    pair_copy = copy(peram_hbm, pair.at[core], send_sem.at[PAIR], pair_recv.at[0], mate)
-    pair_copy.start()
+
+    def pair_copy(part, rows_from):
+        span = pl.ds(rows_from, num_vec - rows_from)
+        return copy(
+            peram_hbm.at[part, span], pair.at[core, part, span], send_sem.at[PAIR], pair_recv.at[part], mate
+        )
+
+    def pair_arrived(part, rows_from):
+        span = pl.ds(rows_from, num_vec - rows_from)
+        there = pair.at[1 - core, part, span]
+        copy(there, there, send_sem.at[PAIR], pair_recv.at[part], mate).wait_recv()
+
+    def each_part(act, first, second):
+        @pl.when(core == 0)
+        def _():
+            for part in range(2):
+                act(part, first)
+
+        @pl.when(core == 1)
+        def _():
+            for part in range(2):
+                act(part, second)
+
+    each_part(lambda part, rows_from: pair_copy(part, rows_from).start(), half, 0)
     load_mom.wait()
     fill_phases(mom_ref, cos_ref, sin_ref, me * local_sites)
     load_own.wait()
     with jax.named_scope("pair"):
-        pair_copy.wait_recv()
+
+        @pl.when(core == 1)
+        def _():
+            pair_arrived(0, half)
+            pair_arrived(1, half)
+
+        @pl.when(core == 0)
+        def _():
+            pair_arrived(0, 0)
+
     mine_rows = pl.ds(pl.multiple_of(core * half, half), half)
     with jax.named_scope("block"):
         lefts = jnp.concatenate([pair[0, 0, mine_rows, :], pair[0, 1, mine_rows, :]], axis=0)
         by_re = dot(lefts, pair[1, 0], NT)
+
+        @pl.when(core == 0)
+        def _():
+            pair_arrived(1, 0)
+
         by_im = dot(lefts, pair[1, 1], NT)
         gath[chip, core, 0] = (by_re[:half] + by_im[half:]).astype(BF16)
         gath[chip, core, 1] = (by_re[half:] - by_im[:half]).astype(BF16)
     def send_own(part):
-        @pl.when(has_above)
-        def _():
-            gather_copy(chip, part, UP, above).start()
-
-        @pl.when(has_below)
-        def _():
-            gather_copy(chip, part, DOWN, below).start()
+        for piece in range(2):
+
+            @pl.when(has_above)
+            def _():
+                gather_copy(chip, part, piece, UP, above).start()
+
+            @pl.when(has_below)
+            def _():
+                gather_copy(chip, part, piece, DOWN, below).start()
+
+    def send_both(block, part, way, to):
+        for piece in range(2):
+            gather_copy(block, part, piece, way, to).start()
+
+    send_both(chip, 0, ACROSS, across)
+    send_own(0)
+    send_both(chip, 1, ACROSS, across)
+
+    @pl.when(jnp.logical_not(at_end))
+    def _():
+        send_own(1)
 
     for part in range(parts):
-        gather_copy(chip, part, ACROSS, across).start()
-    send_own(0)
-
-    @pl.when(jnp.logical_not(at_end))
-    def _():
-        send_own(1)
-
-    for part in range(parts):
-        gather_copy(chip, part, MATE, mate).start()
+        send_both(chip, part, MATE, mate)
 
     def named_product(step, piece):
         with jax.named_scope(f"unit{step}{piece}"):
             product_at(step, piece)
 
-    def named_slot(turn):
-        with jax.named_scope(f"slot{turn}"):
-            slot(turn)
-            relay(turn - 1)
+    def named_slot(turn, piece):
+        with jax.named_scope(f"slot{turn}{piece}"):
+            slot(turn, piece)
+            relay(turn - 1, piece)
 
     with jax.named_scope("load"):
         load_vec.wait()
@@ -477,24 +537,27 @@
     def _():
         send_own(1)
 
-    named_slot(1)
+    named_slot(1, 0)
     named_product(1, 1)
+    named_slot(1, 1)
     named_product(2, 0)
     begin(1, 0)
     begin(1, 1)
-    named_slot(2)
+    named_slot(2, 0)
     named_product(2, 1)
+    named_slot(2, 1)
     named_product(3, 0)
     begin(2, 0)
     begin(2, 1)
-    named_slot(3)
+    named_slot(3, 0)
     named_product(3, 1)
+    named_slot(3, 1)
     load_owner.wait()
     with jax.named_scope("picks"):
         make_picks()
-    named_slot(4)
-    named_slot(5)
-    named_slot(6)
+    for turn in range(4, 7):
+        for piece in range(2):
+            named_slot(turn, piece)
     farthest = nth_line(lines - 1) * wide + column
 
     @pl.when(at_end)
@@ -503,22 +566,28 @@
             line_total(0, send_across)
 
     with jax.named_scope("slot7"):
-        slot(7)
+        for piece in range(2):
+            slot(2 * lines - 1, piece)
+
+            @pl.when(at_end)
+            def _():
+                relay(2 * lines - 2, piece)
 
     @pl.when(at_end)
     def _():
         with jax.named_scope("total1"):
             line_total(1)
-        gather_copy(farthest, 0, ACROSS, across).start()
 
     @pl.when(jnp.logical_not(at_end))
     def _():
         with jax.named_scope("total0"):
-            relay(6)
             line_total(0, send_across)
+        send_both(farthest, 1, ACROSS, across)
+        with jax.named_scope("rel6"):
+            for piece in range(2):
+                relay(2 * lines - 2, piece)
         with jax.named_scope("total1"):
             line_total(1)
-        gather_copy(farthest, 1, ACROSS, across).start()
 
     with jax.named_scope("across"):
         for part, span in spans():
@@ -544,23 +613,35 @@
         by = dot(lhs[1], jnp.concatenate(broad, axis=0), NT)
         put(2 * block + 1, by[:rows], by[rows:])
 
-    @pl.loop(0, 2 * lines)
+    def block_at(turn):
+        return nth_line(turn // 2) * wide + jnp.where(turn % 2 == 0, column, other)
+
+    def relay_last():
+        with jax.named_scope("last"):
+            for piece in range(2):
+                relay(2 * lines - 1, piece)
+
+    @pl.loop(0, lines - 1)
+    def _(pair_turn):
+        @pl.when(at_end & (pair_turn == lines - 2))
+        def _():
+            relay_last()
+
+        first, second = block_at(2 * pair_turn), block_at(2 * pair_turn + 1)
+        with jax.named_scope("mate"):
+            from_mate(first)
+            from_mate(second)
+        with jax.named_scope("contract"):
+            contract(first)
+            contract(second)
+
+    @pl.loop(2 * lines - 2, 2 * lines)
     def _(turn):
-        @pl.when(at_end & (turn == 2 * lines - 3))
-        def _():
-            with jax.named_scope("slot8"):
-                slot(2 * lines)
-                relay(2 * lines - 2)
-
-        @pl.when(turn == jnp.where(at_end, 2 * lines - 1, 2 * lines - 2))
-        def _():
-            with jax.named_scope("last"):
-                relay(2 * lines - 1)
-
-        late = turn >= 2 * lines - 2
-        near = jnp.where(late, turn % 2 == 0, turn < lines - 1)
-        nth = jnp.where(late, lines - 1, turn % (lines - 1))
-        block = nth_line(nth) * wide + jnp.where(near, column, other)
+        @pl.when(jnp.logical_not(at_end) & (turn == 2 * lines - 2))
+        def _():
+            relay_last()
+
+        block = block_at(turn)
         with jax.named_scope("mate"):
             from_mate(block)
         with jax.named_scope("contract"):
@@ -573,7 +654,14 @@
     def all_sent(what, way):
         copy(what, what, send_sem.at[way], core_recv.at[0], mate).wait_send()
 
-    pair_copy.wait_send()
+    @pl.when(core == 0)
+    def _():
+        all_sent(peram_hbm.at[:, pl.ds(half, half)], PAIR)
+
+    @pl.when(core == 1)
+    def _():
+        all_sent(peram_hbm, PAIR)
+
     all_sent(core_out, CORES)
     all_sent(z_out.at[pl.ds(0, lines - 1)], LINES)
     all_sent(y_out, TOTALS)
@@ -628,11 +716,11 @@
             pltpu.VMEM((rows // group, group * fanout, spaces * group), BF16),
             dma((4,)),
             dma((8,)),
-            dma((1,)),
+            dma((2,)),
             dma((chips,)),
             dma((lines + 1, wide, 2)),
             dma((2,)),
-            dma((chips, 2)),
+            dma((chips, 2, 2)),
             dma((chips,)),
         ],
         compiler_params=pltpu.CompilerParams(

time: 43.4 us -> 40.5 us (0.933)
  the two profiles are of different devices: /device:TPU:1 before, /device:TPU:0 now
where the time goes in v3:
time: 40.5 us; the launch traced here: 40.4 us
  Pallas kernels  39.4 us (97%)
  local copies, waits for them, and re-layouts  1.02 us (3%)
    pallas_call x1, Pallas kernels, fused_on_device(): pl.pallas_call(functools.partial(fused_kernel, lines, wide), out_shape=pl...  39.4 us
    unnamed x1, local copies, waits for them, and re-layouts  1.02 us

profile of v3, /device:TPU:0, one launch (start us, length us, event | category | flops | bytes accessed | tf_op | source)
XLA Modules:
  0.0 40.4 jit_solution(4325464634082471991)
XLA Ops:
  0.0 39.4 %shard_map.46 = bf16[96,8,768]{2,1,0:T(8,128)(2,1)S(1)} custom-call(s32[4,3]{1,0:T(4,128)} %mom_hbm.1, bf16[2,3,384,384]{3,2,1,0:T(8,128)(2,1)} %bitcast.3, bf16[2,384,384]{2,1,0:T(8,128)(2,1)} %bitcast.4, s32[8,96]{1,0:T(8,128)} %bitcast.5), custom_call_target="tpu_custom_call" | custom-call | tf_op jit(solution)/shard_map/pallas_call | solution.py:692
  39.4 1.0 %copy.6 = bf16[96,8,768]{2,1,0:T(8,128)(2,1)} copy(bf16[96,8,768]{2,1,0:T(8,128)(2,1)S(1)} %shard_map.46) | data formatting | bytes 2359296

commit v4 on v3

--- a/solution.py
+++ b/solution.py
@@ -325,7 +325,7 @@
         def _():
             gather_copy(block, part, piece, way, to).start()
 
-        @pl.when(jnp.logical_not(held(at, part)))
+        @pl.when(jnp.logical_not(held(at, part, piece)))
         def _():
             gather_copy(block, part, piece, ACROSS, across).start()
 
@@ -354,17 +354,18 @@
         is_sum = (count > 0) & jnp.logical_not(is_block) & (ahead > 0)
         return is_block, is_sum, back, ahead, part
 
-    def held(at, part):
-        return jnp.logical_not(at_end) & (at == line + 2 * toward) & (part == 1)
-
-    def late_sum(turn, count):
-        return (count == lines - 2) & (turn == 2 * lines - 3)
+    def held(at, part, piece):
+        inner = (at == line + 2 * toward) & (part == 1)
+        outer = (at == line + (lines - 1) * toward) & (part == 0)
+        return jnp.where(at_end, outer, inner) if piece else jnp.logical_not(at_end) & inner
+
+    def late_sum(turn, piece, count):
+        return (count == lines - 2) & (turn == 2 * lines - 3) & (piece == 1)
 
     def send_late(way, count, to_line, to):
         @pl.when(count == lines - 2)
         def _():
-            for part in range(2):
-                z_copy(way, to_line, column, part, to).start()
+            z_copy(way, to_line, column, 1, to).start()
 
     def slot(turn, piece):
         is_block, is_sum, back, ahead, part = arrivals(turn, below_count)
@@ -375,7 +376,7 @@
 
         @pl.when(is_sum)
         def _():
-            pass_on(0, line + ahead, part, piece, above, late_sum(turn, below_count))
+            pass_on(0, line + ahead, part, piece, above, late_sum(turn, piece, below_count))
 
         is_block_, is_sum_, back_, ahead_, part_ = arrivals(turn, above_count)
 
@@ -385,7 +386,7 @@
 
         @pl.when(is_sum_)
         def _():
-            pass_on(1, line - ahead_, part_, piece, below, late_sum(turn, above_count))
+            pass_on(1, line - ahead_, part_, piece, below, late_sum(turn, piece, above_count))
 
         if turn == 2 * lines - 2 and piece == 1:
             send_late(0, below_count, lines - 1, above)
@@ -443,9 +444,8 @@
 
     def pair_copy(part, rows_from):
         span = pl.ds(rows_from, num_vec - rows_from)
-        return copy(
-            peram_hbm.at[part, span], pair.at[core, part, span], send_sem.at[PAIR], pair_recv.at[part], mate
-        )
+        there = pair.at[core, part, span]
+        return copy(there, there, send_sem.at[PAIR], pair_recv.at[part], mate)
 
     def pair_arrived(part, rows_from):
         span = pl.ds(rows_from, num_vec - rows_from)
@@ -463,33 +463,37 @@
             for part in range(2):
                 act(part, second)
 
+    load_own.wait()
     each_part(lambda part, rows_from: pair_copy(part, rows_from).start(), half, 0)
     load_mom.wait()
     fill_phases(mom_ref, cos_ref, sin_ref, me * local_sites)
-    load_own.wait()
-    with jax.named_scope("pair"):
-
-        @pl.when(core == 1)
-        def _():
+    def own_lefts():
+        mine_rows = pl.ds(pl.multiple_of(core * half, half), half)
+        return jnp.concatenate([pair[0, 0, mine_rows, :], pair[0, 1, mine_rows, :]], axis=0)
+
+    def own_block(by_re, by_im):
+        gath[chip, core, 0] = (by_re[:half] + by_im[half:]).astype(BF16)
+        gath[chip, core, 1] = (by_re[half:] - by_im[:half]).astype(BF16)
+
+    @pl.when(core == 1)
+    def _():
+        with jax.named_scope("pair"):
             pair_arrived(0, half)
             pair_arrived(1, half)
-
-        @pl.when(core == 0)
-        def _():
+        with jax.named_scope("block"):
+            lefts = own_lefts()
+            own_block(dot(lefts, pair[1, 0], NT), dot(lefts, pair[1, 1], NT))
+
+    @pl.when(core == 0)
+    def _():
+        with jax.named_scope("pair"):
             pair_arrived(0, 0)
-
-    mine_rows = pl.ds(pl.multiple_of(core * half, half), half)
-    with jax.named_scope("block"):
-        lefts = jnp.concatenate([pair[0, 0, mine_rows, :], pair[0, 1, mine_rows, :]], axis=0)
-        by_re = dot(lefts, pair[1, 0], NT)
-
-        @pl.when(core == 0)
-        def _():
+        with jax.named_scope("block"):
+            lefts = own_lefts()
+            by_re = dot(lefts, pair[1, 0], NT)
             pair_arrived(1, 0)
-
-        by_im = dot(lefts, pair[1, 1], NT)
-        gath[chip, core, 0] = (by_re[:half] + by_im[half:]).astype(BF16)
-        gath[chip, core, 1] = (by_re[half:] - by_im[:half]).astype(BF16)
+            own_block(by_re, dot(lefts, pair[1, 1], NT))
+
     def send_own(part):
         for piece in range(2):
 
@@ -558,6 +562,10 @@
     for turn in range(4, 7):
         for piece in range(2):
             named_slot(turn, piece)
+    def send_held(part, span):
+        if part == 0:
+            gather_copy(farthest, 1, 0, ACROSS, across).start()
+
     farthest = nth_line(lines - 1) * wide + column
 
     @pl.when(at_end)
@@ -569,12 +577,9 @@
         for piece in range(2):
             slot(2 * lines - 1, piece)
 
-            @pl.when(at_end)
-            def _():
-                relay(2 * lines - 2, piece)
-
     @pl.when(at_end)
     def _():
+        relay(2 * lines - 2, 0)
         with jax.named_scope("total1"):
             line_total(1)
 
@@ -582,12 +587,24 @@
     def _():
         with jax.named_scope("total0"):
             line_total(0, send_across)
-        send_both(farthest, 1, ACROSS, across)
         with jax.named_scope("rel6"):
             for piece in range(2):
                 relay(2 * lines - 2, piece)
+        inward = (line - toward) * wide + other
+        outward = (line + 2 * toward) * wide + other
+
+        @pl.when(lower)
+        def _():
+            gather_copy(inward, 1, 1, UP, above).start()
+            gather_copy(outward, 0, 1, DOWN, below).start()
+
+        @pl.when(jnp.logical_not(lower))
+        def _():
+            gather_copy(inward, 1, 1, DOWN, below).start()
+            gather_copy(outward, 0, 1, UP, above).start()
+
         with jax.named_scope("total1"):
-            line_total(1)
+            line_total(1, send_held)
 
     with jax.named_scope("across"):
         for part, span in spans():
@@ -618,29 +635,25 @@
 
     def relay_last():
         with jax.named_scope("last"):
+
+            @pl.when(at_end)
+            def _():
+                relay(2 * lines - 2, 1)
+
             for piece in range(2):
                 relay(2 * lines - 1, piece)
 
-    @pl.loop(0, lines - 1)
-    def _(pair_turn):
-        @pl.when(at_end & (pair_turn == lines - 2))
-        def _():
-            relay_last()
-
-        first, second = block_at(2 * pair_turn), block_at(2 * pair_turn + 1)
-        with jax.named_scope("mate"):
-            from_mate(first)
-            from_mate(second)
-        with jax.named_scope("contract"):
-            contract(first)
-            contract(second)
+    early = [block_at(turn) for turn in range(2 * lines - 2)]
+    with jax.named_scope("mate"):
+        for block in early:
+            from_mate(block)
+    with jax.named_scope("contract"):
+        for block in early:
+            contract(block)
+    relay_last()
 
     @pl.loop(2 * lines - 2, 2 * lines)
     def _(turn):
-        @pl.when(jnp.logical_not(at_end) & (turn == 2 * lines - 2))
-        def _():
-            relay_last()
-
         block = block_at(turn)
         with jax.named_scope("mate"):
             from_mate(block)
@@ -656,26 +669,30 @@
 
     @pl.when(core == 0)
     def _():
-        all_sent(peram_hbm.at[:, pl.ds(half, half)], PAIR)
+        all_sent(pair.at[0, :, pl.ds(half, half)], PAIR)
 
     @pl.when(core == 1)
     def _():
-        all_sent(peram_hbm, PAIR)
+        all_sent(pair.at[1], PAIR)
 
     all_sent(core_out, CORES)
     all_sent(z_out.at[pl.ds(0, lines - 1)], LINES)
     all_sent(y_out, TOTALS)
-    all_sent(gath.at[pl.ds(0, lines), core], ACROSS)
     all_sent(gath.at[:, core], MATE)
+
+    def pieces_sent(count, way):
+        all_sent(results.at[pl.ds(0, half // (4 * group)), pl.ds(0, count)], way)
+
+    pieces_sent(4 * lines - 1, ACROSS)
     for count in range(1, lines):
 
         @pl.when(line == count - 1)
         def _():
-            all_sent(gath.at[pl.ds(0, count), core], UP)
+            pieces_sent(4 * count + (1 if count > 1 else 0), UP)
 
         @pl.when(line == lines - count)
         def _():
-            all_sent(gath.at[pl.ds(0, count), core], DOWN)
+            pieces_sent(4 * count + (1 if count > 1 else 0), DOWN)
 
 
 def fused_on_device(eigvecs, momenta, peram, graph):

time: 40.5 us -> 39.2 us (0.968)
  Pallas kernels: 39.4 us -> 38 us
    pallas_call x1, Pallas kernels: 39.4 us -> 38 us  [fused_on_device(): pl.pallas_call(functools.partial(fused_kernel, lines, wide), out_shape=pl...]
where the time goes in v4:
time: 39.2 us; the launch traced here: 39.1 us
  Pallas kernels  38 us (97%)
  local copies, waits for them, and re-layouts  1.02 us (3%)
    pallas_call x1, Pallas kernels, fused_on_device(): pl.pallas_call(functools.partial(fused_kernel, lines, wide), out_shape=pl...  38 us
    unnamed x1, local copies, waits for them, and re-layouts  1.02 us

profile of v4, /device:TPU:0, one launch (start us, length us, event | category | flops | bytes accessed | tf_op | source)
XLA Modules:
  0.0 39.1 jit_solution(10705502111097468193)
XLA Ops:
  0.0 38.0 %shard_map.46 = bf16[96,8,768]{2,1,0:T(8,128)(2,1)S(1)} custom-call(s32[4,3]{1,0:T(4,128)} %mom_hbm.1, bf16[2,3,384,384]{3,2,1,0:T(8,128)(2,1)} %bitcast.3, bf16[2,384,384]{2,1,0:T(8,128)(2,1)} %bitcast.4, s32[8,96]{1,0:T(8,128)} %bitcast.5), custom_call_target="tpu_custom_call" | custom-call | tf_op jit(solution)/shard_map/pallas_call | solution.py:709
  38.0 1.0 %copy.6 = bf16[96,8,768]{2,1,0:T(8,128)(2,1)} copy(bf16[96,8,768]{2,1,0:T(8,128)(2,1)S(1)} %shard_map.46) | data formatting | bytes 2359296

commit v5 on v4

--- a/solution.py
+++ b/solution.py
@@ -144,9 +144,9 @@
 
 
 def fused_kernel(
-    lines, wide, mom_hbm, vec_hbm, peram_hbm, owner_hbm, out_ref,
+    lines, wide, mom_hbm, vec_hbm, peram_hbm, owner_hbm, results, picks,
     mom_ref, vec_ref, owner_ref, cos_ref, sin_ref, pair, gath, prod, own, core_out, core_in, z_out, z_in, total, y_out, y_in,
-    lhs, results, picks, load_sem, send_sem, pair_recv, core_recv, z_recv, y_recv, gath_recv, mate_recv,
+    lhs, load_sem, send_sem, pair_recv, core_recv, z_recv, y_recv, gath_recv, mate_recv,
 ):
     colours, num_vec, local_sites = vec_ref.shape[1:]
     rows = own.shape[1]
@@ -307,15 +307,23 @@
 
     def gather_copy(block, part, piece, way, to):
         there = gath.at[block, core, part, pl.ds(piece * (half // 2), half // 2)]
-        recv = mate_recv.at[block] if way == MATE else gath_recv.at[block, part, piece]
+        recv = mate_recv.at[mate_place(block)] if way == MATE else gath_recv.at[block, part, piece]
         return copy(there, there, send_sem.at[way], recv, to)
 
     def gather_arrived(block, part, piece):
         gather_copy(block, part, piece, ACROSS, across).wait_recv()
 
+    def mate_place(block):
+        far = line + toward * jnp.where(at_end, lines - 1, 2)
+        return jnp.where(block // wide != far, 0, jnp.where(block % wide == column, 1, 2))
+
     def from_mate(block):
         there = gath.at[block, 1 - core]
-        copy(there, there, send_sem.at[MATE], mate_recv.at[block], mate).wait_recv()
+        copy(there, there, send_sem.at[MATE], mate_recv.at[mate_place(block)], mate).wait_recv()
+
+    def early_from_mate():
+        there = gath.at[pl.ds(0, wide * (lines - 1)), 1 - core]
+        copy(there, there, send_sem.at[MATE], mate_recv.at[0], mate).wait_recv()
 
     def spread(at, part, piece, onward, way, to):
         block = at * wide + column
@@ -419,7 +427,7 @@
         y_copy(part, span).start()
 
     group = results.shape[2]
-    fanout = out_ref.shape[1]
+    fanout = owner_ref.shape[0]
     owners = results.shape[1]
 
     def make_picks():
@@ -494,31 +502,25 @@
             pair_arrived(1, 0)
             own_block(by_re, dot(lefts, pair[1, 1], NT))
 
-    def send_own(part):
-        for piece in range(2):
-
-            @pl.when(has_above)
-            def _():
-                gather_copy(chip, part, piece, UP, above).start()
-
-            @pl.when(has_below)
-            def _():
-                gather_copy(chip, part, piece, DOWN, below).start()
-
-    def send_both(block, part, way, to):
-        for piece in range(2):
-            gather_copy(block, part, piece, way, to).start()
-
-    send_both(chip, 0, ACROSS, across)
-    send_own(0)
-    send_both(chip, 1, ACROSS, across)
-
-    @pl.when(jnp.logical_not(at_end))
-    def _():
-        send_own(1)
-
-    for part in range(parts):
-        send_both(chip, part, MATE, mate)
+    def send_own(part, piece):
+        @pl.when(has_above)
+        def _():
+            gather_copy(chip, part, piece, UP, above).start()
+
+        @pl.when(has_below)
+        def _():
+            gather_copy(chip, part, piece, DOWN, below).start()
+
+    for piece in range(2):
+        send_own(0, piece)
+        gather_copy(chip, 0, piece, ACROSS, across).start()
+    for piece in range(2):
+
+        @pl.when(jnp.logical_not(at_end))
+        def _():
+            send_own(1, piece)
+
+        gather_copy(chip, 1, piece, ACROSS, across).start()
 
     def named_product(step, piece):
         with jax.named_scope(f"unit{step}{piece}"):
@@ -537,9 +539,14 @@
     named_product(1, 0)
     begin(0, 1)
 
-    @pl.when(at_end)
-    def _():
-        send_own(1)
+    for piece in range(2):
+
+        @pl.when(at_end)
+        def _():
+            send_own(1, piece)
+
+        for part in range(parts):
+            gather_copy(chip, part, piece, MATE, mate).start()
 
     named_slot(1, 0)
     named_product(1, 1)
@@ -645,24 +652,20 @@
 
     early = [block_at(turn) for turn in range(2 * lines - 2)]
     with jax.named_scope("mate"):
-        for block in early:
-            from_mate(block)
+        early_from_mate()
     with jax.named_scope("contract"):
         for block in early:
             contract(block)
     relay_last()
 
-    @pl.loop(2 * lines - 2, 2 * lines)
-    def _(turn):
+    def contract_at(turn):
         block = block_at(turn)
         with jax.named_scope("mate"):
             from_mate(block)
         with jax.named_scope("contract"):
             contract(block)
 
-    for g in range(rows // group):
-        rows_out = dot(picks[g], results[g].reshape(owners * group, 2 * num_vec), NN)
-        out_ref[g * group : (g + 1) * group] = rows_out.reshape(group, fanout, 2 * num_vec).astype(BF16)
+    contract_at(2 * lines - 2)
 
     def all_sent(what, way):
         copy(what, what, send_sem.at[way], core_recv.at[0], mate).wait_send()
@@ -678,7 +681,6 @@
     all_sent(core_out, CORES)
     all_sent(z_out.at[pl.ds(0, lines - 1)], LINES)
     all_sent(y_out, TOTALS)
-    all_sent(gath.at[:, core], MATE)
 
     def pieces_sent(count, way):
         all_sent(results.at[pl.ds(0, half // (4 * group)), pl.ds(0, count)], way)
@@ -693,6 +695,22 @@
         @pl.when(line == lines - count)
         def _():
             pieces_sent(4 * count + (1 if count > 1 else 0), DOWN)
+
+    contract_at(2 * lines - 1)
+    all_sent(gath.at[:, core], MATE)
+
+def pick_kernel(results, picks, out_hbm, out, sems):
+    groups, owners, group, width = results.shape
+    fanout = out.shape[1]
+    copies = []
+    for g in range(groups):
+        part = slice(g * group, (g + 1) * group)
+        picked = dot(picks[g], results[g].reshape(owners * group, width), NN)
+        out[part] = picked.reshape(group, fanout, width).astype(BF16)
+        copies.append(pltpu.make_async_copy(out.at[part], out_hbm.at[part], sems.at[g]))
+        copies[-1].start()
+    for each in copies:
+        each.wait()
 
 
 def fused_on_device(eigvecs, momenta, peram, graph):
@@ -706,11 +724,15 @@
     vectors = jnp.transpose(eigvecs, (0, 2, 1, 3))
     half = num_vec // 2
     dma = pltpu.SemaphoreType.DMA
-    return pl.pallas_call(
+    groups = rows // group
+    results, picks = pl.pallas_call(
         functools.partial(fused_kernel, lines, wide),
-        out_shape=pltpu.VMEM((rows, fanout, 2 * num_vec), BF16),
+        out_shape=(
+            pltpu.VMEM((groups, spaces, group, 2 * num_vec), BF16),
+            pltpu.VMEM((groups, group * fanout, spaces * group), BF16),
+        ),
         in_specs=[pl.BlockSpec(memory_space=pltpu.HBM)] * 4,
-        out_specs=pl.BlockSpec(memory_space=pltpu.VMEM),
+        out_specs=[pl.BlockSpec(memory_space=pltpu.VMEM)] * 2,
         scratch_shapes=[
             pltpu.SMEM(momenta.shape, jnp.int32),
             pltpu.VMEM((2, colours, num_vec, local_sites), BF16),
@@ -729,8 +751,6 @@
             pltpu.VMEM((rows, 2 * num_vec), BF16),
             pltpu.VMEM((rows, 2 * num_vec), BF16),
             pltpu.VMEM((2, 2 * rows, 2 * num_vec), BF16),
-            pltpu.VMEM((rows // group, spaces, group, 2 * num_vec), BF16),
-            pltpu.VMEM((rows // group, group * fanout, spaces * group), BF16),
             dma((4,)),
             dma((8,)),
             dma((2,)),
@@ -738,12 +758,22 @@
             dma((lines + 1, wide, 2)),
             dma((2,)),
             dma((chips, 2, 2)),
-            dma((chips,)),
+            dma((3,)),
         ],
         compiler_params=pltpu.CompilerParams(
             collective_id=0, has_side_effects=True, vmem_limit_bytes=VMEM_ROOM + (16 << 20)
         ),
     )(momenta, vectors, peram[0], graph.T)
+    return pl.pallas_call(
+        pick_kernel,
+        out_shape=jax.ShapeDtypeStruct((rows, fanout, 2 * num_vec), BF16),
+        in_specs=[pl.BlockSpec(memory_space=pltpu.VMEM)] * 2,
+        out_specs=pl.BlockSpec(memory_space=pltpu.HBM),
+        scratch_shapes=[pltpu.VMEM((rows, fanout, 2 * num_vec), BF16), dma((groups,))],
+    )(
+        pltpu.with_memory_space_constraint(results, pltpu.VMEM),
+        pltpu.with_memory_space_constraint(picks, pltpu.VMEM),
+    )
 
 
 def fits(mesh, eigvecs, momenta, graph):

time: 39.2 us -> 39.1 us (level)
  local copies, waits for them, and re-layouts: 1.02 us -> 0 us
  Pallas kernels: 38 us -> 38.8 us
    unnamed x1 -> x0, local copies, waits for them, and re-layouts: 1.02 us -> none
    pallas_call x1 -> x2, Pallas kernels: 38 us -> 38.8 us  [the longest x1 37.5 us: fused_on_device(): pl.pallas_call(functools.partial(fused_kernel, lines, wide), out_shape=(p...]
where the time goes in v5:
time: 39.1 us; the launch traced here: 39 us
  Pallas kernels  38.8 us (99%)
    pallas_call x1, Pallas kernels, fused_on_device(): pl.pallas_call(functools.partial(fused_kernel, lines, wide), out_shape=(p...  37.5 us
    pallas_call x1, Pallas kernels, fused_on_device(): pl.pallas_call(pick_kernel, out_shape=jax.ShapeDtypeStruct((rows, fanout,...  1.29 us

profile of v5, /device:TPU:0, one launch (start us, length us, event | category | flops | bytes accessed | tf_op | source)
XLA Modules:
  0.0 39.0 jit_solution(8204965477924001973)
XLA Ops:
  0.0 37.5 %shard_map.46 = (bf16[6,16,16,768]{3,2,1,0:T(8,128)(2,1)S(1)}, bf16[6,128,256]{2,1,0:T(8,128)(2,1)S(1)}) custom-call(s32[4,3]{1,0:T(4,128)} %mom_hbm.1, bf16[2,3,384,384]{3,2,1,0:T(8,128)(2,1)} %bitcast.3, bf16[2,384,384]{2,1,0:T(8,128)(2,1)} %bitcast.4, s32[8,96]{1,0:T(8,128)} %bitcast.5), custom_call_target="tpu_custom_call" | custom-call | tf_op jit(solution)/shard_map/pallas_call | solution.py:728
  37.5 1.3 %shard_map.47 = bf16[96,8,768]{2,1,0:T(8,128)(2,1)} custom-call(bf16[6,16,16,768]{3,2,1,0:T(8,128)(2,1)S(1)} %get-tuple-element.7.results, bf16[6,128,256]{2,1,0:T(8,128)(2,1)S(1)} %get-tuple-element.8.picks), custom_call_target="tpu_custom_call" | custom-call | tf_op jit(solution)/shard_map/pallas_call | solution.py:767

commit v6 on v5

--- a/solution.py
+++ b/solution.py
@@ -192,9 +192,9 @@
             [(mom_hbm, mom_ref), (peram_hbm, pair.at[core]), (vec_hbm, vec_ref), (owner_hbm, owner_ref)]
         )
     ]
-    for load in loads:
-        load.start()
     load_mom, load_own, load_vec, load_owner = loads
+    load_own.start()
+    load_mom.start()
     UP, ACROSS, MATE, DOWN, CORES, LINES, TOTALS, PAIR = range(8)
 
     def core_copy(unit):
@@ -447,6 +447,9 @@
             picks[g] = jnp.where(same & chosen, 1.0, 0.0).astype(BF16)
 
     peers = 2 + jnp.where(has_above, 1, 0) + jnp.where(has_below, 1, 0)
+    load_own.wait()
+    load_vec.start()
+    load_owner.start()
     with jax.named_scope("greet"):
         pl.semaphore_wait(barrier, peers)
 
@@ -471,7 +474,6 @@
             for part in range(2):
                 act(part, second)
 
-    load_own.wait()
     each_part(lambda part, rows_from: pair_copy(part, rows_from).start(), half, 0)
     load_mom.wait()
     fill_phases(mom_ref, cos_ref, sin_ref, me * local_sites)

time: 39.1 us -> 39.1 us (level)
  no operation moved by 1% of the time
where the time goes in v6:
time: 39.1 us; the launch traced here: 39 us
  Pallas kernels  38.8 us (99%)
    pallas_call x1, Pallas kernels, fused_on_device(): pl.pallas_call(functools.partial(fused_kernel, lines, wide), out_shape=(p...  37.5 us
    pallas_call x1, Pallas kernels, fused_on_device(): pl.pallas_call(pick_kernel, out_shape=jax.ShapeDtypeStruct((rows, fanout,...  1.29 us

profile of v6, /device:TPU:0, one launch (start us, length us, event | category | flops | bytes accessed | tf_op | source)
XLA Modules:
  0.0 39.0 jit_solution(4801136850736230595)
XLA Ops:
  0.0 37.5 %shard_map.46 = (bf16[6,16,16,768]{3,2,1,0:T(8,128)(2,1)S(1)}, bf16[6,128,256]{2,1,0:T(8,128)(2,1)S(1)}) custom-call(s32[4,3]{1,0:T(4,128)} %mom_hbm.1, bf16[2,3,384,384]{3,2,1,0:T(8,128)(2,1)} %bitcast.3, bf16[2,384,384]{2,1,0:T(8,128)(2,1)} %bitcast.4, s32[8,96]{1,0:T(8,128)} %bitcast.5), custom_call_target="tpu_custom_call" | custom-call | tf_op jit(solution)/shard_map/pallas_call | solution.py:730
  37.5 1.3 %shard_map.47 = bf16[96,8,768]{2,1,0:T(8,128)(2,1)} custom-call(bf16[6,16,16,768]{3,2,1,0:T(8,128)(2,1)S(1)} %get-tuple-element.7.results, bf16[6,128,256]{2,1,0:T(8,128)(2,1)S(1)} %get-tuple-element.8.picks), custom_call_target="tpu_custom_call" | custom-call | tf_op jit(solution)/shard_map/pallas_call | solution.py:769

commit v7 on v5

--- a/solution.py
+++ b/solution.py
@@ -643,12 +643,13 @@
     def relay_last():
         with jax.named_scope("last"):
 
+            relay(2 * lines - 1, 0)
+
             @pl.when(at_end)
             def _():
                 relay(2 * lines - 2, 1)
 
-            for piece in range(2):
-                relay(2 * lines - 1, piece)
+            relay(2 * lines - 1, 1)
 
     early = [block_at(turn) for turn in range(2 * lines - 2)]
     with jax.named_scope("mate"):

time: 39.1 us -> 39.1 us (level)
  no operation moved by 1% of the time
where the time goes in v7:
time: 39.1 us; the launch traced here: 39 us
  Pallas kernels  38.8 us (99%)
    pallas_call x1, Pallas kernels, fused_on_device(): pl.pallas_call(functools.partial(fused_kernel, lines, wide), out_shape=(p...  37.5 us
    pallas_call x1, Pallas kernels, fused_on_device(): pl.pallas_call(pick_kernel, out_shape=jax.ShapeDtypeStruct((rows, fanout,...  1.29 us

profile of v7, /device:TPU:0, one launch (start us, length us, event | category | flops | bytes accessed | tf_op | source)
XLA Modules:
  0.0 39.0 jit_solution(2750202896135627585)
XLA Ops:
  0.0 37.5 %shard_map.46 = (bf16[6,16,16,768]{3,2,1,0:T(8,128)(2,1)S(1)}, bf16[6,128,256]{2,1,0:T(8,128)(2,1)S(1)}) custom-call(s32[4,3]{1,0:T(4,128)} %mom_hbm.1, bf16[2,3,384,384]{3,2,1,0:T(8,128)(2,1)} %bitcast.3, bf16[2,384,384]{2,1,0:T(8,128)(2,1)} %bitcast.4, s32[8,96]{1,0:T(8,128)} %bitcast.5), custom_call_target="tpu_custom_call" | custom-call | tf_op jit(solution)/shard_map/pallas_call | solution.py:729
  37.5 1.3 %shard_map.47 = bf16[96,8,768]{2,1,0:T(8,128)(2,1)} custom-call(bf16[6,16,16,768]{3,2,1,0:T(8,128)(2,1)S(1)} %get-tuple-element.7.results, bf16[6,128,256]{2,1,0:T(8,128)(2,1)S(1)} %get-tuple-element.8.picks), custom_call_target="tpu_custom_call" | custom-call | tf_op jit(solution)/shard_map/pallas_call | solution.py:768
